TPU v7x, 128 devices: a whole 4x4x4 slice. The times are simulated.
128 devices in a mesh: row: 4 (over y), col: 16 (over x, z_lo, core), depth: 2 (over z_hi).
Axes of the slice: x: 4, y: 4, z: 4 (z_hi: 2, z_lo: 2; z = z_hi * 2 + z_lo), core: 2. Of those that a mesh axis runs over, the one named last changes fastest.
Arguments:
- sequence_stack: bfloat16 [256, 384, 64], P('depth', ('row', 'col')), may hold values from -6 to 6
- present_sequence_flags: int32 [256], replicated, may hold values 0 or 1
- genuine_residue_flags: int32 [384], replicated, may hold values 0 or 1
- couple_state: bfloat16 [384, 384, 128], P('row', 'col'), may hold values from -6 to 6
- tensor_scale: float32 [64], replicated, may hold values from 0.1 to 1.9
- tensor_entry_matrix: bfloat16 [64, 64], replicated, may hold values from -0.75 to 0.75
- tensor_final_matrix: bfloat16 [1024, 128], replicated, may hold values from -1 to 1
- tensor_offset: float32 [128], replicated, may hold values from -3 to 3
- mean_sequence_scale: float32 [64], replicated, may hold values from 0.1 to 1.9
- mean_couple_scale: float32 [128], replicated, may hold values from 0.1 to 1.9
- mean_score_matrix: float32 [128, 8], replicated, may hold values from -64 to 64
- mean_content_matrix: bfloat16 [64, 256], replicated, may hold values from -0.75 to 0.75
- mean_sigmoid_matrix: bfloat16 [64, 256], replicated, may hold values from -0.75 to 0.75
- mean_final_matrix: bfloat16 [256, 64], replicated, may hold values from -0.375 to 0.375
- trimul_scale: float32 [128], replicated, may hold values from 0.1 to 1.9
- trimul_entry_matrix: bfloat16 [128, 640], replicated, may hold values from -0.5 to 0.5
- trimul_result_scale: float32 [128], replicated, may hold values from 0.1 to 1.9
- trimul_final_matrix: bfloat16 [128, 128], replicated, may hold values from -0.5 to 0.5
Outputs:
- revised_sequences: bfloat16 [256, 384, 64], P('depth', ('row', 'col'))
- pair_output: bfloat16 [384, 384, 128], P('row', 'col')
All inputs are finite; a program needn't handle non-finite values.
Results may differ from a plain program's by a relative error of at most 0.012.
The roundings to bfloat16 on the way count: a program that leaves them out, or rounds other values in their place, can miss the bound.
Values may be sent and summed in bfloat16 or wider, within the bound.
A program may use at most 128 MiB of HBM per device.

v0:
```python
import jax
import jax.numpy as jnp
from jax import lax
from jax.sharding import PartitionSpec as P

epsilon = 1e-05


def sent_to_all(array, axis):
    size = lax.axis_size(axis)
    return lax.all_to_all(
        jnp.broadcast_to(array[None], (size, *array.shape)), axis, 0, 0, tiled=True
    )


def laid_out(tiles, dim):
    shape = list(tiles.shape[1:])
    shape[dim] *= tiles.shape[0]
    return jnp.moveaxis(tiles, 0, dim).reshape(shape)


def gathered_copies(array, axis, dim):
    tiles = sent_to_all(array, axis)
    return laid_out(tiles, dim)


def broadcast(array, axis, root):
    return lax.dynamic_index_in_dim(lax.all_gather(array, axis), root, 0, keepdims=False)


def taken_together(array, axis):
    return sent_to_all(array, axis).sum(axis=0)


def taken_together_2(array, axis):
    everything = sent_to_all(array, axis)
    return jnp.max(everything, axis=0)


def split_up(array, dim, size):
    before, after = (array.shape[:dim], array.shape[dim + 1 :])
    return jnp.moveaxis(array.reshape(*before, size, -1, *after), dim, 0)


def sum_at_owner(array, axis, dim):
    size = lax.axis_size(axis)
    tiles = lax.all_to_all(split_up(array, dim, size), axis, 0, 0, tiled=True)
    return jnp.sum(tiles.astype(jnp.float32), axis=0)


def standardize_features(value_rows, scale):
    value_rows = value_rows.astype(jnp.float32)
    average = jnp.mean(value_rows, -1, keepdims=True)
    centred = value_rows - average
    variance = jnp.mean(centred * centred, -1, keepdims=True)
    return centred * lax.rsqrt(variance + epsilon) * scale


def on_device(
    sequence_stack,
    present_sequence_flags,
    genuine_residue_flags,
    couple_state,
    tensor_scale,
    tensor_entry_matrix,
    tensor_final_matrix,
    tensor_offset,
    mean_sequence_scale,
    mean_couple_scale,
    mean_score_matrix,
    mean_content_matrix,
    mean_sigmoid_matrix,
    mean_final_matrix,
    trimul_scale,
    trimul_entry_matrix,
    trimul_result_scale,
    trimul_final_matrix,
):
    n_row = lax.axis_size("row")
    n_col = lax.axis_size("col")
    row_index = lax.axis_index("row")
    col_index = lax.axis_index("col")
    depth_position = lax.axis_index("depth")
    piece_rows, piece_columns, width = couple_state.shape
    sequence_count, shard_residues, ignored_quantity = sequence_stack.shape
    hidden = tensor_entry_matrix.shape[1] // 2
    head_split = mean_score_matrix.shape[1]
    head_channels = mean_content_matrix.shape[1] // head_split
    token_weight = genuine_residue_flags.astype(jnp.float32)
    mask_as_float = present_sequence_flags.astype(jnp.float32)
    row_softmax_weight = lax.dynamic_slice_in_dim(
        mask_as_float, depth_position * sequence_count, sequence_count
    )
    row_count = jnp.sum(mask_as_float)
    entire_sequences = gathered_copies(sequence_stack, "col", 1)
    root_row = col_index * n_row // n_col
    offset = col_index * piece_columns - root_row * piece_rows
    column_piece = lax.dynamic_slice_in_dim(entire_sequences, offset, piece_columns, 1)
    whole_cols = broadcast(column_piece, "row", root_row)
    opm_rows = standardize_features(entire_sequences, tensor_scale).astype(jnp.bfloat16)
    opm_cols = standardize_features(whole_cols, tensor_scale).astype(jnp.bfloat16)
    left_projection = (
        jnp.dot(opm_rows, tensor_entry_matrix[:, :hidden], preferred_element_type=jnp.float32)
        * row_softmax_weight[:, None, None]
    ).astype(jnp.bfloat16)
    right_proj = (
        jnp.dot(opm_cols, tensor_entry_matrix[:, hidden:], preferred_element_type=jnp.float32)
        * row_softmax_weight[:, None, None]
    ).astype(jnp.bfloat16)
    outer_sum = jnp.einsum(
        "sic,sjd->ijcd", left_projection, right_proj, preferred_element_type=jnp.float32
    )
    outer_sum = outer_sum.reshape(piece_rows, piece_columns, hidden * hidden)
    out_float = tensor_final_matrix.astype(jnp.float32)
    partial_proj = jnp.dot(outer_sum, out_float, precision=lax.Precision.HIGHEST)
    projected_total = taken_together(partial_proj, "depth")
    update = projected_total / (row_count + 0.001) + tensor_offset
    pair_one = (couple_state.astype(jnp.float32) + update).astype(jnp.bfloat16)
    row_tokens = lax.dynamic_slice_in_dim(token_weight, row_index * piece_rows, piece_rows)
    col_tokens = lax.dynamic_slice_in_dim(token_weight, col_index * piece_columns, piece_columns)
    logits = jnp.einsum(
        "ijc,ch->ijh",
        standardize_features(pair_one, mean_couple_scale),
        mean_score_matrix,
        precision=lax.Precision.HIGHEST,
    )
    logits = logits + 1000000000.0 * (col_tokens - 1.0)[None, :, None]
    peak = taken_together_2(jnp.max(logits, axis=1), "col")
    expo = jnp.exp(logits - peak[:, None, :])
    total = taken_together(jnp.sum(expo, axis=1), "col")
    weights = (expo / total[:, None, :]).astype(jnp.bfloat16)
    col_normed = standardize_features(whole_cols, mean_sequence_scale).astype(jnp.bfloat16)
    value_rows = jnp.dot(
        col_normed, mean_content_matrix, preferred_element_type=jnp.float32
    ).astype(jnp.bfloat16)
    value_rows = value_rows.reshape(sequence_count, piece_columns, head_split, head_channels)
    averaged_values = jnp.einsum(
        "ijh,sjhe->sihe", weights, value_rows, preferred_element_type=jnp.float32
    )
    averaged_values = averaged_values.reshape(
        sequence_count, piece_rows, head_split * head_channels
    )
    output_weight = mean_final_matrix.astype(jnp.float32)
    row_normed = standardize_features(entire_sequences, mean_sequence_scale).astype(jnp.bfloat16)
    gate_values = jax.nn.sigmoid(
        jnp.dot(row_normed, mean_sigmoid_matrix, preferred_element_type=jnp.float32)
    )
    partial_update = jnp.dot(
        gate_values * averaged_values, output_weight, precision=lax.Precision.HIGHEST
    )
    sequence_delta = sum_at_owner(partial_update.astype(jnp.bfloat16), "col", 1)
    revised_sequences = (sequence_stack.astype(jnp.float32) + sequence_delta).astype(jnp.bfloat16)
    tri_normed = standardize_features(pair_one, trimul_scale).astype(jnp.bfloat16)
    projected = jnp.dot(tri_normed, trimul_entry_matrix, preferred_element_type=jnp.float32)
    pair_mask = (row_tokens[:, None] * col_tokens[None, :])[..., None]
    tri_left = (
        jax.nn.sigmoid(projected[..., 0:width]) * projected[..., width : 2 * width] * pair_mask
    ).astype(jnp.bfloat16)
    tri_right = (
        jax.nn.sigmoid(projected[..., 2 * width : 3 * width])
        * projected[..., 3 * width : 4 * width]
        * pair_mask
    ).astype(jnp.bfloat16)
    out_gate = jax.nn.sigmoid(projected[..., 4 * width : 5 * width])
    right_all = gathered_copies(tri_right, "row", 0)
    partial_product = jnp.einsum(
        "ikc,jkc->ijc", tri_left, right_all, preferred_element_type=jnp.float32
    )
    product = lax.psum_scatter(
        partial_product.astype(jnp.bfloat16), "col", scatter_dimension=1, tiled=True
    ).astype(jnp.float32)
    final = out_gate * jnp.dot(
        standardize_features(product, trimul_result_scale).astype(jnp.bfloat16),
        trimul_final_matrix,
        preferred_element_type=jnp.float32,
    )
    pair_output = (pair_one.astype(jnp.float32) + final).astype(jnp.bfloat16)
    return (revised_sequences, pair_output)


def solution(mesh):
    placed = (
        P("depth", ("row", "col"), None),
        P(),
        P(),
        P("row", "col", None),
        P(),
        P(),
        P(),
        P(),
        P(),
        P(),
        P(),
        P(),
        P(),
        P(),
        P(),
        P(),
        P(),
        P(),
    )
    return jax.shard_map(
        on_device,
        mesh=mesh,
        in_specs=placed,
        out_specs=(P("depth", ("row", "col"), None), P("row", "col", None)),
        check_vma=False,
    )
```

profile of v0, /device:TPU:1, one launch (start us, length us, event | category | flops | bytes accessed | tf_op | source)
XLA Modules:
  0.0 340.3 jit_solution(1035658563237114094)
XLA Ops:
  9.7 7.3 %all-to-all-start = ((bf16[16,128,6,64]{1,3,2,0:T(8,128)(2,1)}), bf16[16,128,6,64]{1,3,2,0:T(8,128)(2,1)S(1)}, u32[]{:S(2)}, u32[]{:S(2)}) async-start(bf16[16,128,6,64]{1,3,2,0:T(8,128)(2,1)} %broadcast_in_dim.10), calls=%async_computation | async-start | bytes 3145728 | tf_op jit(solution)/shard_map/all_to_all | solution.py:11
  17.0 21.3 %all-to-all-done = bf16[16,128,6,64]{1,3,2,0:T(8,128)(2,1)S(1)} async-done(((bf16[16,128,6,64]{1,3,2,0:T(8,128)(2,1)}), bf16[16,128,6,64]{1,3,2,0:T(8,128)(2,1)S(1)}, u32[]{:S(2)}, u32[]{:S(2)}) %all-to-all-start) | async-done | bytes 1572896 | tf_op jit(solution)/shard_map/all_to_all | solution.py:11
  41.2 28.2 %all-gather.3.cloned.1.call-done = bf16[512,24,64]{0,2,1:T(8,128)(2,1)} async-done(((bf16[128,24,64]{0,2,1:T(8,128)(2,1)}), bf16[512,24,64]{0,2,1:T(8,128)(2,1)}) %all-gather.3.cloned.1.call-update) | async-done | bytes 1572880 | tf_op jit(solution)/shard_map/all_gather | solution.py:28
  69.4 3.5 %reshape.137 = bf16[4,128,24,64]{1,0,3,2:T(4,128)(2,1)} reshape(bf16[512,24,64]{0,2,1:T(8,128)(2,1)} %all-gather.3.cloned.1.call-done) | data formatting | bytes 3145728 | tf_op jit(solution)/shard_map/all_gather | solution.py:28
  75.6 7.3 %fusion.48 = f32[24,32,96,32]{2,1,3,0:T(8,128)} fusion(bf16[128,96,32]{0,2,1:T(8,128)(2,1)S(1)} %multiply_convert_fusion.4, f32[128,24,64]{0,2,1:T(8,128)S(1)} %bitcast.79, f32[64]{0:T(128)S(1)} %copy-done.13, f32[128,24]{0,1:T(8,128)S(1)} %add_rsqrt_fusion.3, f32[128,24]{0,1:T(8,128)S(1)} %broadcast_multiply_fusion.4, f32[128]{0:T(128)} %copy-done.14, ...), kind=kOutput, calls=%fused_computation.68 | convolution fusion | flops 617545728 | bytes 11043584 | tf_op jit(solution)/shard_map/sic,sjd->ijcd/dot_general | solution.py:110
  82.9 13.0 %fusion.70 = f32[96,24,128]{2,0,1:T(8,128)S(1)} fusion(f32[96,24,1024]{0,2,1:T(8,128)} %bitcast.73, bf16[1024,128]{1,0:T(8,128)(2,1)S(1)} %copy-done), kind=kOutput, calls=%fused_computation.92 | convolution fusion | flops 3623878656 | bytes 10878976 | tf_op jit(solution)/shard_map/dot_general | solution.py:115
  98.1 5.2 %all-to-all-start.1 = ((f32[2,96,24,128]{3,2,1,0:T(8,128)}), f32[2,96,24,128]{3,2,1,0:T(8,128)}, u32[]{:S(2)}, u32[]{:S(2)}) async-start(f32[2,96,24,128]{3,2,1,0:T(8,128)} %broadcast_in_dim.11), calls=%async_computation.1 | async-start | bytes 4718592 | tf_op jit(solution)/shard_map/all_to_all | solution.py:11
  104.8 26.3 %all-to-all-done.1 = f32[2,96,24,128]{3,2,1,0:T(8,128)} async-done(((f32[2,96,24,128]{3,2,1,0:T(8,128)}), f32[2,96,24,128]{3,2,1,0:T(8,128)}, u32[]{:S(2)}, u32[]{:S(2)}) %all-to-all-start.1) | async-done | bytes 2359328 | tf_op jit(solution)/shard_map/all_to_all | solution.py:11
  131.1 3.0 reduce_sum.120
  142.8 4.5 %all-to-all-start.5 = ((bf16[4,96,24,128]{3,2,1,0:T(8,128)(2,1)}), bf16[4,96,24,128]{3,2,1,0:T(8,128)(2,1)}, u32[]{:S(2)}, u32[]{:S(2)}) async-start(bf16[4,96,24,128]{3,2,1,0:T(8,128)(2,1)} %broadcast_in_dim.14), calls=%async_computation.5 | async-start | bytes 4718592 | tf_op jit(solution)/shard_map/all_to_all | solution.py:11
  149.9 24.3 %all-to-all-done.5 = bf16[4,96,24,128]{3,2,1,0:T(8,128)(2,1)} async-done(((bf16[4,96,24,128]{3,2,1,0:T(8,128)(2,1)}), bf16[4,96,24,128]{3,2,1,0:T(8,128)(2,1)}, u32[]{:S(2)}, u32[]{:S(2)}) %all-to-all-start.5) | async-done | bytes 2359328 | tf_op jit(solution)/shard_map/all_to_all | solution.py:11
  174.2 4.8 %copy.149 = bf16[384,24,128]{0,1,2:T(8,128)(2,1)} copy(bf16[384,24,128]{2,1,0:T(8,128)(2,1)} %bitcast.24) | data formatting | bytes 4718592 | tf_op jit(solution)/shard_map/reshape | solution.py:19
  179.0 8.1 %convert_bitcast_fusion = bf16[96,384,128]{1,0,2:T(8,128)(2,1)} fusion(bf16[384,24,128]{0,1,2:T(8,128)(2,1)} %copy.149, bf16[96,24,128]{0,1,2:T(8,128)(2,1)} %copy.150), kind=kOutput, calls=%fused_computation.6 | convolution fusion | flops 231211008 | bytes 12386304 | tf_op jit(solution)/shard_map/ikc,jkc->ijc/dot_general | solution.py:166
  187.1 13.9 %copy.151 = bf16[96,384,128]{2,0,1:T(8,128)(2,1)} copy(bf16[96,384,128]{1,0,2:T(8,128)(2,1)} %convert_bitcast_fusion) | data formatting | bytes 18874368 | tf_op jit(solution)/shard_map/convert_element_type | solution.py:170
  201.7 6.9 %fusion.90 = (f32[96,8]{1,0:T(8,128)S(1)}, f32[96,24,8]{1,2,0:T(8,128)}) fusion(f32[24]{0:T(128)S(1)} %get-tuple-element.2, f32[128,8]{0,1:T(8,128)S(1)} %copy-done.20, bf16[96,24,128]{2,1,0:T(8,128)(2,1)S(1)} %get-tuple-element.5, f32[128]{0:T(128)S(1)} %copy-done.21, f32[96,24]{1,0:T(8,128)S(1)} %copy.140, f32[96,24]{1,0:T(8,128)S(1)} %copy.138), kind=kOutput, calls=%fused_computation.123 | convolution fusion | flops 29527296 | bytes 689760 | tf_op jit(solution)/shard_map/ijc,ch->ijh/dot_general | solution.py:121
  209.4 8.3 %all-to-all-start.2 = ((f32[16,96,8]{1,2,0:T(8,128)}), f32[16,96,8]{1,2,0:T(8,128)S(1)}, u32[]{:S(2)}, u32[]{:S(2)}) async-start(f32[16,96,8]{1,2,0:T(8,128)} %broadcast_in_dim.12), calls=%async_computation.2 | async-start | bytes 131072 | tf_op jit(solution)/shard_map/all_to_all | solution.py:11
  217.6 6.5 %fusion.12 = f32[128,96,256]{2,0,1:T(8,128)} fusion(bf16[128,96,64]{0,2,1:T(8,128)(2,1)S(1)} %bitcast.77, f32[64]{0:T(128)S(1)} %copy-done.11, f32[128,96]{0,1:T(8,128)S(1)} %rsqrt.39, f32[128,96]{0,1:T(8,128)S(1)} %div.67, bf16[64,256]{1,0:T(8,128)(2,1)S(1)} %copy-done.7), kind=kOutput, calls=%fused_computation.21 | convolution fusion | flops 406585344 | bytes 14287104 | tf_op jit(solution)/shard_map/dot_general | solution.py:146
  226.3 5.7 %all-to-all-start.3 = ((f32[16,96,8]{1,2,0:T(8,128)}), f32[16,96,8]{1,2,0:T(8,128)S(1)}, u32[]{:S(2)}, u32[]{:S(2)}) async-start(f32[16,96,8]{1,2,0:T(8,128)} %broadcast_in_dim.13), calls=%async_computation.3 | async-start | bytes 131072 | tf_op jit(solution)/shard_map/all_to_all | solution.py:11
  238.3 6.3 %fusion.72 = f32[8,128,32,96]{1,3,2,0:T(8,128)} fusion(bf16[128,24,8,32]{0,1,3,2:T(8,128)(2,1)S(1)} %bitcast.81, bf16[96,24,8,1]{1,2,0,3:T(8,128)(2,1)S(1)} %fusion.75), kind=kOutput, calls=%fused_computation.94 | convolution fusion | flops 150994944 | bytes 14192640 | tf_op jit(solution)/shard_map/ijh,sjhe->sihe/dot_general | solution.py:137
  244.6 12.8 %copy.148 = f32[128,96,256]{2,0,1:T(8,128)} copy(f32[128,96,256]{0,1,2:T(8,128)} %bitcast.74) | data formatting | bytes 25165824 | tf_op jit(solution)/shard_map/reshape | solution.py:140
  257.5 14.8 %fusion.9 = bf16[128,96,64]{0,2,1:T(8,128)(2,1)S(1)} fusion(f32[128,96,256]{2,0,1:T(8,128)} %copy.148, f32[128,96,256]{2,0,1:T(8,128)} %fusion.12, bf16[256,64]{0,1:T(8,128)(2,1)S(1)} %copy-done.18), kind=kOutput, calls=%fused_computation.20 | convolution fusion | flops 2429288448 | bytes 26771456 | tf_op jit(solution)/shard_map/dot_general | solution.py:148
  272.3 28.6 %all_to_all.30 = bf16[16,128,6,64]{1,3,2,0:T(8,128)(2,1)S(1)} all-to-all(bf16[16,128,6,64]{1,3,2,0:T(8,128)(2,1)S(1)} %bitcast.82), channel_id=1, replica_groups=mesh['row'=4,'col'=16,'depth'=2] {'col'}, dimensions={0} | all-to-all | bytes 3145728 | tf_op jit(solution)/shard_map/all_to_all | solution.py:47
  302.4 24.2 %reduce-scatter.2.cloned.1.call-done = bf16[96,24,128]{2,0,1:T(8,128)(2,1)} async-done(((bf16[96,384,128]{2,0,1:T(8,128)(2,1)}), bf16[96,24,128]{2,0,1:T(8,128)(2,1)}) %reduce-scatter.2.cloned.1.call-update) | async-done | bytes 589840 | tf_op jit(solution)/shard_map/reduce_scatter | solution.py:169
  330.8 2.7 fusion.26
  (103 shorter events, 37.7 us)
Async XLA Ops:
  7.2 75.7 %copy-start = (bf16[1024,128]{1,0:T(8,128)(2,1)S(1)}, bf16[1024,128]{1,0:T(8,128)(2,1)}, u32[]{:S(2)}) copy-start(bf16[1024,128]{1,0:T(8,128)(2,1)} %param.24) | copy-start | bytes 786436
  9.7 29.4 %copy-start.12 = (s32[256]{0:T(256)S(1)}, s32[256]{0:T(256)}, u32[]{:S(2)}) copy-start(s32[256]{0:T(256)} %param.19) | copy-start | bytes 3076
  9.7 28.6 %all-to-all-start = ((bf16[16,128,6,64]{1,3,2,0:T(8,128)(2,1)}), bf16[16,128,6,64]{1,3,2,0:T(8,128)(2,1)S(1)}, u32[]{:S(2)}, u32[]{:S(2)}) async-start(bf16[16,128,6,64]{1,3,2,0:T(8,128)(2,1)} %broadcast_in_dim.10), calls=%async_computation | async-start | bytes 3145728 | tf_op jit(solution)/shard_map/all_to_all | solution.py:11
  17.0 52.5 %all-gather.3.cloned.1.call-start = ((), (), s32[]{:S(2)}) async-start(), calls=%async_computation.8 | async-start | bytes 1966080 | tf_op jit(solution)/shard_map/all_gather | solution.py:28
  39.2 1.3 copy-start.13
  98.1 5.2 %copy-start.10 = (s32[384]{0:T(512)S(1)}, s32[384]{0:T(512)}, u32[]{:S(2)}) copy-start(s32[384]{0:T(512)} %param.20) | copy-start | bytes 4612
  98.1 33.0 %all-to-all-start.1 = ((f32[2,96,24,128]{3,2,1,0:T(8,128)}), f32[2,96,24,128]{3,2,1,0:T(8,128)}, u32[]{:S(2)}, u32[]{:S(2)}) async-start(f32[2,96,24,128]{3,2,1,0:T(8,128)} %broadcast_in_dim.11), calls=%async_computation.1 | async-start | bytes 4718592 | tf_op jit(solution)/shard_map/all_to_all | solution.py:11
  104.8 29.2 %copy-start.15 = (f32[128]{0:T(128)S(1)}, f32[128]{0:T(128)}, u32[]{:S(2)}) copy-start(f32[128]{0:T(128)} %param.25) | copy-start | bytes 1540
  134.0 2.9 copy-start.6
  134.0 2.9 copy-start.17
  138.5 2.7 copy-start.2
  142.8 31.4 %all-to-all-start.5 = ((bf16[4,96,24,128]{3,2,1,0:T(8,128)(2,1)}), bf16[4,96,24,128]{3,2,1,0:T(8,128)(2,1)}, u32[]{:S(2)}, u32[]{:S(2)}) async-start(bf16[4,96,24,128]{3,2,1,0:T(8,128)(2,1)} %broadcast_in_dim.14), calls=%async_computation.5 | async-start | bytes 4718592 | tf_op jit(solution)/shard_map/all_to_all | solution.py:11
  147.3 179.3 %reduce-scatter.2.cloned.1.call-start = ((), (), s32[]{:S(2)}) async-start(), calls=%async_computation.7 | async-start | bytes 10027008 | tf_op jit(solution)/shard_map/reduce_scatter | solution.py:169
  201.1 16.6 %copy-start.7 = (bf16[64,256]{1,0:T(8,128)(2,1)S(1)}, bf16[64,256]{1,0:T(8,128)(2,1)}, u32[]{:S(2)}) copy-start(bf16[64,256]{1,0:T(8,128)(2,1)} %param.30) | copy-start | bytes 98308
  201.1 16.6 %copy-start.11 = (f32[64]{0:T(128)S(1)}, f32[64]{0:T(128)}, u32[]{:S(2)}) copy-start(f32[64]{0:T(128)} %param.26) | copy-start | bytes 772
  209.4 14.8 %all-to-all-start.2 = ((f32[16,96,8]{1,2,0:T(8,128)}), f32[16,96,8]{1,2,0:T(8,128)S(1)}, u32[]{:S(2)}, u32[]{:S(2)}) async-start(f32[16,96,8]{1,2,0:T(8,128)} %broadcast_in_dim.12), calls=%async_computation.2 | async-start | bytes 131072 | tf_op jit(solution)/shard_map/all_to_all | solution.py:11
  217.6 14.4 %copy-start.8 = (bf16[64,256]{1,0:T(8,128)(2,1)S(1)}, bf16[64,256]{1,0:T(8,128)(2,1)}, u32[]{:S(2)}) copy-start(bf16[64,256]{1,0:T(8,128)(2,1)} %param.29) | copy-start | bytes 98308
  226.3 11.6 %all-to-all-start.3 = ((f32[16,96,8]{1,2,0:T(8,128)}), f32[16,96,8]{1,2,0:T(8,128)S(1)}, u32[]{:S(2)}, u32[]{:S(2)}) async-start(f32[16,96,8]{1,2,0:T(8,128)} %broadcast_in_dim.13), calls=%async_computation.3 | async-start | bytes 131072 | tf_op jit(solution)/shard_map/all_to_all | solution.py:11
  233.9 4.1 %copy-start.4 = (f32[96,24,8]{1,2,0:T(8,128)S(1)}, f32[96,24,8]{1,2,0:T(8,128)}, u32[]{:S(2)}) copy-start(f32[96,24,8]{1,2,0:T(8,128)} %get-tuple-element.11) | copy-start | bytes 221188
  244.6 12.8 %copy-start.18 = (bf16[256,64]{0,1:T(8,128)(2,1)S(1)}, bf16[256,64]{0,1:T(8,128)(2,1)}, u32[]{:S(2)}) copy-start(bf16[256,64]{0,1:T(8,128)(2,1)} %param.31) | copy-start | bytes 98308
  300.9 29.0 %copy-start.16 = (f32[128]{0:T(128)S(1)}, f32[128]{0:T(128)}, u32[]{:S(2)}) copy-start(f32[128]{0:T(128)} %param.34) | copy-start | bytes 1540
  301.8 29.0 %copy-start.19 = (bf16[128,128]{1,0:T(8,128)(2,1)S(1)}, bf16[128,128]{1,0:T(8,128)(2,1)}, u32[]{:S(2)}) copy-start(bf16[128,128]{1,0:T(8,128)(2,1)} %param.35) | copy-start | bytes 98308
  326.6 3.3 copy-start.3
  330.8 2.7 copy-start.1
  (5 other events, 4.8 us)
Sparse Core Ops, SparseCore 0:
  39.2 30.1 all-gather.2
  201.2 125.3 reduce-scatter.1
where the time goes:
time: 342 us; the launch traced here: 340 us
  waiting for transfers between devices  126 us (37%)
  matrix products  69.8 us (20%)
  local copies, waits for them, and re-layouts  50.8 us (15%)
  starting transfers between devices  31.1 us (9%)
  blocking collectives  28.6 us (8%)
  other arithmetic  18.7 us (5%)
  between operations  15.1 us (4%)
    all_to_all x5, waiting for transfers between devices, sent_to_all(): lax.all_to_all(jnp.broadcast_to(array[None], (size, *array.shape)), axis,...  73.8 us
    all_to_all x5, starting transfers between devices, sent_to_all(): lax.all_to_all(jnp.broadcast_to(array[None], (size, *array.shape)), axis,...  31 us
    all_to_all x1, blocking collectives, sum_at_owner(): tiles = lax.all_to_all(split_up(array, dim, size), axis, 0, 0, tiled=True)  28.6 us
    all_gather x1, waiting for transfers between devices, broadcast(): lax.all_gather(array, axis)  28.2 us
    reduce_scatter x1, waiting for transfers between devices, on_device(): lax.psum_scatter(partial_product.astype(jnp.bfloat16), 'col', scatter_dim...  24.2 us
    dot_general x1, matrix products, on_device(): jnp.dot(gate_values * averaged_values, output_weight, precision=lax.Preci...  14.8 us
    convert_element_type x1, local copies, waits for them, and re-layouts, on_device(): partial_product.astype(jnp.bfloat16)  13.9 us
    dot_general x1, matrix products, on_device(): jnp.dot(outer_sum, out_float, precision=lax.Precision.HIGHEST)  13 us
  transfers between devices with their start and end apart: 7, of which 6 were waited for; matrix products, arithmetic and copies ran while one was open for 18% of the time, Pallas kernels for 0%

commit v1 on v0

--- a/solution.py
+++ b/solution.py
@@ -162,13 +162,23 @@
         * pair_mask
     ).astype(jnp.bfloat16)
     out_gate = jax.nn.sigmoid(projected[..., 4 * width : 5 * width])
-    right_all = gathered_copies(tri_right, "row", 0)
-    partial_product = jnp.einsum(
-        "ikc,jkc->ijc", tri_left, right_all, preferred_element_type=jnp.float32
-    )
-    product = lax.psum_scatter(
-        partial_product.astype(jnp.bfloat16), "col", scatter_dimension=1, tiled=True
-    ).astype(jnp.float32)
+    axes = ("row", "col", "depth")
+    n_depth = lax.axis_size("depth")
+    half = piece_columns // n_depth
+    both = jnp.stack([tri_left, tri_right], axis=0)
+    both = lax.dynamic_slice_in_dim(both, depth_position * half, half, 2)
+    by_channel = jnp.transpose(both, (3, 2, 0, 1))
+    arrived = lax.all_to_all(by_channel, axes, 0, 0, tiled=True)
+    arrived = arrived.reshape(n_row, n_col * n_depth * half, 2, piece_rows)
+    channel_product = jnp.einsum(
+        "akm,bkn->ambn", arrived[:, :, 0], arrived[:, :, 1], preferred_element_type=jnp.float32
+    ).astype(jnp.bfloat16)
+    channel_product = channel_product.reshape(n_row, piece_rows, n_col, piece_columns)
+    outgoing = jnp.transpose(channel_product, (0, 2, 1, 3))[:, :, None]
+    outgoing = jnp.broadcast_to(outgoing, (n_row, n_col, n_depth, piece_rows, piece_columns))
+    outgoing = outgoing.reshape(n_row * n_col * n_depth, piece_rows, piece_columns)
+    returned = lax.all_to_all(outgoing, axes, 0, 0, tiled=True)
+    product = jnp.transpose(returned, (1, 2, 0)).astype(jnp.float32)
     final = out_gate * jnp.dot(
         standardize_features(product, trimul_result_scale).astype(jnp.bfloat16),
         trimul_final_matrix,

time: 342 us -> 261 us (0.76)
  waiting for transfers between devices: 126 us -> 82.5 us
  blocking collectives: 28.6 us -> 0 us
  starting transfers between devices: 31.1 us -> 46.3 us
  local copies, waits for them, and re-layouts: 50.8 us -> 36.1 us
  matrix products: 69.8 us -> 62.2 us
    all_to_all x5 -> x4, waiting for transfers between devices: 73.8 us -> 40.9 us  [sent_to_all(): lax.all_to_all(jnp.broadcast_to(array[None], (size, *array.shape)), axis,...]
    all_to_all x1 -> x0, blocking collectives: 28.6 us -> none  [sum_at_owner(): tiles = lax.all_to_all(split_up(array, dim, size), axis, 0, 0, tiled=True)]
    reduce_scatter x1 -> x0, waiting for transfers between devices: 24.2 us -> none  [on_device(): lax.psum_scatter(partial_product.astype(jnp.bfloat16), 'col', scatter_dim...]
    all_to_all x0 -> x3, starting transfers between devices: none -> 20.5 us  [the longest x1 9.76 us: on_device(): returned = lax.all_to_all(outgoing, axes, 0, 0, tiled=True)]
    all_to_all x0 -> x3, waiting for transfers between devices: none -> 15.3 us  [the longest x1 15.1 us: sum_at_owner(): tiles = lax.all_to_all(split_up(array, dim, size), axis, 0, 0, tiled=True)]
    convert_element_type x2, local copies, waits for them, and re-layouts: 16.4 us -> 1.97 us  [the longest x1 1.75 us: on_device(): standardize_features(product, trimul_result_scale).astype(jnp.bfloat16)]
    dot_general x1, matrix products: 8.11 us -> 0.39 us  [on_device(): jnp.einsum('akm,bkn->ambn', arrived[:, :, 0], arrived[:, :, 1], preferred...]
    all_to_all x5 -> x4, starting transfers between devices: 31 us -> 25.7 us  [sent_to_all(): lax.all_to_all(jnp.broadcast_to(array[None], (size, *array.shape)), axis,...]
  transfers between devices with their start and end apart: 7 -> 8, of which waited for: 6 -> 7; matrix products, arithmetic and copies ran while one was open for 18% -> 24% of each run, Pallas kernels for 0% -> 0%
where the time goes in v1:
time: 261 us; the launch traced here: 260 us
  waiting for transfers between devices  82.5 us (32%)
  matrix products  62.2 us (24%)
  starting transfers between devices  46.3 us (18%)
  local copies, waits for them, and re-layouts  36.1 us (14%)
  other arithmetic  17.4 us (7%)
  between operations  15.2 us (6%)
    all_to_all x4, waiting for transfers between devices, sent_to_all(): lax.all_to_all(jnp.broadcast_to(array[None], (size, *array.shape)), axis,...  40.9 us
    all_gather x1, waiting for transfers between devices, broadcast(): lax.all_gather(array, axis)  26.3 us
    all_to_all x4, starting transfers between devices, sent_to_all(): lax.all_to_all(jnp.broadcast_to(array[None], (size, *array.shape)), axis,...  25.7 us
    dot_general x1, matrix products, on_device(): jnp.dot(gate_values * averaged_values, output_weight, precision=lax.Preci...  15.9 us
    all_to_all x1, waiting for transfers between devices, sum_at_owner(): tiles = lax.all_to_all(split_up(array, dim, size), axis, 0, 0, tiled=True)  15.1 us
    dot_general x1, matrix products, on_device(): jnp.dot(outer_sum, out_float, precision=lax.Precision.HIGHEST)  13 us
    reshape x1, local copies, waits for them, and re-layouts, on_device(): averaged_values.reshape(sequence_count, piece_rows, head_split * head_cha...  12.7 us
    all_to_all x1, starting transfers between devices, on_device(): returned = lax.all_to_all(outgoing, axes, 0, 0, tiled=True)  9.76 us
  transfers between devices with their start and end apart: 8, of which 7 were waited for; matrix products, arithmetic and copies ran while one was open for 24% of the time, Pallas kernels for 0%

profile of v1, /device:TPU:1, one launch (start us, length us, event | category | flops | bytes accessed | tf_op | source)
XLA Modules:
  0.0 259.6 jit_solution(16017834254769920707)
XLA Ops:
  7.2 2.5 broadcast_in_dim.10
  9.7 7.3 %all-to-all-start = ((bf16[16,128,6,64]{1,3,2,0:T(8,128)(2,1)}), bf16[16,128,6,64]{1,3,2,0:T(8,128)(2,1)S(1)}, u32[]{:S(2)}, u32[]{:S(2)}) async-start(bf16[16,128,6,64]{1,3,2,0:T(8,128)(2,1)} %broadcast_in_dim.10), calls=%async_computation | async-start | bytes 3145728 | tf_op jit(solution)/shard_map/all_to_all | solution.py:11
  17.0 21.3 %all-to-all-done = bf16[16,128,6,64]{1,3,2,0:T(8,128)(2,1)S(1)} async-done(((bf16[16,128,6,64]{1,3,2,0:T(8,128)(2,1)}), bf16[16,128,6,64]{1,3,2,0:T(8,128)(2,1)S(1)}, u32[]{:S(2)}, u32[]{:S(2)}) %all-to-all-start) | async-done | bytes 1572896 | tf_op jit(solution)/shard_map/all_to_all | solution.py:11
  43.2 26.3 %all-gather.3.cloned.1.call-done = bf16[512,24,64]{0,2,1:T(8,128)(2,1)} async-done(((bf16[128,24,64]{0,2,1:T(8,128)(2,1)}), bf16[512,24,64]{0,2,1:T(8,128)(2,1)}) %all-gather.3.cloned.1.call-update) | async-done | bytes 1572880 | tf_op jit(solution)/shard_map/all_gather | solution.py:28
  69.4 3.5 %reshape.145 = bf16[4,128,24,64]{1,0,3,2:T(4,128)(2,1)} reshape(bf16[512,24,64]{0,2,1:T(8,128)(2,1)} %all-gather.3.cloned.1.call-done) | data formatting | bytes 3145728 | tf_op jit(solution)/shard_map/all_gather | solution.py:28
  72.9 2.5 fusion.94
  75.6 7.3 %fusion.50 = f32[24,32,96,32]{2,1,3,0:T(8,128)} fusion(bf16[128,96,32]{0,2,1:T(8,128)(2,1)S(1)} %multiply_convert_fusion.4, f32[128,24,64]{0,2,1:T(8,128)S(1)} %bitcast.109, f32[64]{0:T(128)S(1)} %copy-done.13, f32[128,24]{0,1:T(8,128)S(1)} %add_rsqrt_fusion.3, f32[128,24]{0,1:T(8,128)S(1)} %broadcast_multiply_fusion.4, f32[128]{0:T(128)} %copy-done.14, ...), kind=kOutput, calls=%fused_computation.72 | convolution fusion | flops 617545728 | bytes 11043584 | tf_op jit(solution)/shard_map/sic,sjd->ijcd/dot_general | solution.py:110
  82.9 13.0 %fusion.75 = f32[96,24,128]{2,0,1:T(8,128)S(1)} fusion(f32[96,24,1024]{0,2,1:T(8,128)} %bitcast.103, bf16[1024,128]{1,0:T(8,128)(2,1)S(1)} %copy-done), kind=kOutput, calls=%fused_computation.99 | convolution fusion | flops 3623878656 | bytes 10878976 | tf_op jit(solution)/shard_map/dot_general | solution.py:115
  98.1 5.3 %all-to-all-start.1 = ((f32[2,96,24,128]{3,2,1,0:T(8,128)}), f32[2,96,24,128]{3,2,1,0:T(8,128)}, u32[]{:S(2)}, u32[]{:S(2)}) async-start(f32[2,96,24,128]{3,2,1,0:T(8,128)} %broadcast_in_dim.11), calls=%async_computation.1 | async-start | bytes 4718592 | tf_op jit(solution)/shard_map/all_to_all | solution.py:11
  103.6 6.5 %fusion.12 = f32[128,96,256]{2,0,1:T(8,128)} fusion(bf16[128,96,64]{0,2,1:T(8,128)(2,1)S(1)} %bitcast.107, f32[64]{0:T(128)S(1)} %copy-done.11, f32[128,96]{0,1:T(8,128)S(1)} %rsqrt.39, f32[128,96]{0,1:T(8,128)S(1)} %div.67, bf16[64,256]{1,0:T(8,128)(2,1)S(1)} %copy-done.7), kind=kOutput, calls=%fused_computation.20 | convolution fusion | flops 406585344 | bytes 14287104 | tf_op jit(solution)/shard_map/dot_general | solution.py:146
  113.9 17.0 %all-to-all-done.1 = f32[2,96,24,128]{3,2,1,0:T(8,128)} async-done(((f32[2,96,24,128]{3,2,1,0:T(8,128)}), f32[2,96,24,128]{3,2,1,0:T(8,128)}, u32[]{:S(2)}, u32[]{:S(2)}) %all-to-all-start.1) | async-done | bytes 2359328 | tf_op jit(solution)/shard_map/all_to_all | solution.py:11
  130.9 3.0 %reduce_sum.120 = f32[96,24,128]{2,1,0:T(8,128)} reduce(f32[2,96,24,128]{3,2,1,0:T(8,128)} %all-to-all-done.1, f32[]{:T(128)} %constant.25.clone.1), dimensions={0}, to_apply=%region_4.5 | reduce | flops 294912 | bytes 3538948 | tf_op jit(solution)/shard_map/reduce_sum | solution.py:32
  136.7 6.0 %fusion.96 = (f32[96,8]{1,0:T(8,128)S(1)}, f32[96,24,8]{1,2,0:T(8,128)S(1)}) fusion(f32[24]{0:T(128)S(1)} %get-tuple-element.2, f32[128,8]{0,1:T(8,128)S(1)} %copy-done.21, bf16[96,24,128]{2,1,0:T(8,128)(2,1)S(1)} %get-tuple-element.5, f32[128]{0:T(128)S(1)} %copy-done.22, f32[96,24]{1,0:T(8,128)S(1)} %copy.127, f32[96,24]{1,0:T(8,128)S(1)} %copy.125), kind=kOutput, calls=%fused_computation.131 | convolution fusion | flops 29527296 | bytes 689760 | tf_op jit(solution)/shard_map/ijc,ch->ijh/dot_general | solution.py:121
  143.5 7.7 %all-to-all-start.2 = ((f32[16,96,8]{1,2,0:T(8,128)}), f32[16,96,8]{1,2,0:T(8,128)S(1)}, u32[]{:S(2)}, u32[]{:S(2)}) async-start(f32[16,96,8]{1,2,0:T(8,128)} %broadcast_in_dim.12), calls=%async_computation.2 | async-start | bytes 131072 | tf_op jit(solution)/shard_map/all_to_all | solution.py:11
  152.7 2.5 copy-done.2
  158.2 5.4 %all-to-all-start.3 = ((f32[16,96,8]{1,2,0:T(8,128)}), f32[16,96,8]{1,2,0:T(8,128)S(1)}, u32[]{:S(2)}, u32[]{:S(2)}) async-start(f32[16,96,8]{1,2,0:T(8,128)} %broadcast_in_dim.13), calls=%async_computation.3 | async-start | bytes 131072 | tf_op jit(solution)/shard_map/all_to_all | solution.py:11
  169.5 5.1 %all-to-all-start.5 = ((bf16[128,12,2,96]{3,2,1,0:T(2,128)(2,1)}), bf16[128,12,2,96]{3,2,1,0:T(2,128)(2,1)S(1)}, u32[]{:S(2)}, u32[]{:S(2)}) async-start(bf16[128,12,2,96]{3,2,1,0:T(2,128)(2,1)} %copy.136), calls=%async_computation.5 | async-start | bytes 1572864 | tf_op jit(solution)/shard_map/all_to_all | solution.py:171
  176.1 6.3 %fusion.77 = f32[8,128,32,96]{1,3,2,0:T(8,128)} fusion(bf16[128,24,8,32]{0,1,3,2:T(8,128)(2,1)S(1)} %bitcast.112, bf16[96,24,8,1]{1,2,0,3:T(8,128)(2,1)S(1)} %fusion.80), kind=kOutput, calls=%fused_computation.101 | convolution fusion | flops 150994944 | bytes 14192640 | tf_op jit(solution)/shard_map/ijh,sjhe->sihe/dot_general | solution.py:137
  182.4 12.7 %copy.135 = f32[128,96,256]{2,0,1:T(8,128)} copy(f32[128,96,256]{0,1,2:T(8,128)} %bitcast.104) | data formatting | bytes 25165824 | tf_op jit(solution)/shard_map/reshape | solution.py:140
  198.9 9.8 %all-to-all-start.6 = ((bf16[128,96,24]{1,2,0:T(8,128)(2,1)}), bf16[128,96,24]{1,2,0:T(8,128)(2,1)S(1)}, u32[]{:S(2)}, u32[]{:S(2)}) async-start(bf16[128,96,24]{1,2,0:T(8,128)(2,1)} %bitcast.35), calls=%async_computation.6 | async-start | bytes 1572864 | tf_op jit(solution)/shard_map/all_to_all | solution.py:180
  208.7 15.9 %fusion.9 = bf16[128,96,64]{0,2,1:T(8,128)(2,1)} fusion(f32[128,96,256]{2,0,1:T(8,128)} %copy.135, f32[128,96,256]{2,0,1:T(8,128)} %fusion.12, bf16[256,64]{0,1:T(8,128)(2,1)S(1)} %copy-done.19), kind=kOutput, calls=%fused_computation.19 | convolution fusion | flops 2429288448 | bytes 26771456 | tf_op jit(solution)/shard_map/dot_general | solution.py:148
  224.9 5.6 %all-to-all-start.4 = ((bf16[16,128,6,64]{1,3,2,0:T(8,128)(2,1)}), bf16[16,128,6,64]{1,3,2,0:T(8,128)(2,1)S(1)}, u32[]{:S(2)}, u32[]{:S(2)}) async-start(bf16[16,128,6,64]{1,3,2,0:T(8,128)(2,1)} %bitcast.113), calls=%async_computation.4 | async-start | bytes 3145728 | tf_op jit(solution)/shard_map/all_to_all | solution.py:47
  234.1 2.6 %fusion.29 = bf16[96,24,128]{2,1,0:T(8,128)(2,1)} fusion(bf16[96,24,128]{2,1,0:T(8,128)(2,1)S(1)} %copy.140, bf16[96,24,128]{2,1,0:T(8,128)(2,1)S(1)} %get-tuple-element.5, f32[96,24,640]{2,1,0:T(8,128)} %copy-done.2, bf16[128,128]{1,0:T(8,128)(2,1)S(1)} %copy-done.20), kind=kOutput, calls=%fused_computation.41 | convolution fusion | flops 77561856 | bytes 2981888 | tf_op jit(solution)/shard_map/dot_general | solution.py:182
  236.7 15.1 %all-to-all-done.4 = bf16[16,128,6,64]{1,3,2,0:T(8,128)(2,1)S(1)} async-done(((bf16[16,128,6,64]{1,3,2,0:T(8,128)(2,1)}), bf16[16,128,6,64]{1,3,2,0:T(8,128)(2,1)S(1)}, u32[]{:S(2)}, u32[]{:S(2)}) %all-to-all-start.4) | async-done | bytes 1572896 | tf_op jit(solution)/shard_map/all_to_all | solution.py:47
  (109 shorter events, 34.3 us)
Async XLA Ops:
  7.2 75.7 %copy-start = (bf16[1024,128]{1,0:T(8,128)(2,1)S(1)}, bf16[1024,128]{1,0:T(8,128)(2,1)}, u32[]{:S(2)}) copy-start(bf16[1024,128]{1,0:T(8,128)(2,1)} %param.24) | copy-start | bytes 786436
  9.7 29.4 %copy-start.12 = (s32[256]{0:T(256)S(1)}, s32[256]{0:T(256)}, u32[]{:S(2)}) copy-start(s32[256]{0:T(256)} %param.19) | copy-start | bytes 3076
  9.7 29.5 %copy-start.10 = (s32[384]{0:T(512)S(1)}, s32[384]{0:T(512)}, u32[]{:S(2)}) copy-start(s32[384]{0:T(512)} %param.20) | copy-start | bytes 4612
  9.7 28.6 %all-to-all-start = ((bf16[16,128,6,64]{1,3,2,0:T(8,128)(2,1)}), bf16[16,128,6,64]{1,3,2,0:T(8,128)(2,1)S(1)}, u32[]{:S(2)}, u32[]{:S(2)}) async-start(bf16[16,128,6,64]{1,3,2,0:T(8,128)(2,1)} %broadcast_in_dim.10), calls=%async_computation | async-start | bytes 3145728 | tf_op jit(solution)/shard_map/all_to_all | solution.py:11
  17.0 52.5 %all-gather.3.cloned.1.call-start = ((), (), s32[]{:S(2)}) async-start(), calls=%async_computation.7 | async-start | bytes 1966080 | tf_op jit(solution)/shard_map/all_gather | solution.py:28
  39.2 3.2 %copy-start.14 = (f32[128]{0:T(128)}, f32[128]{0:T(128)S(1)}, u32[]{:S(2)}) copy-start(f32[128]{0:T(128)S(1)} %dynamic_slice.21) | copy-start | bytes 1540
  98.1 5.4 %copy-start.17 = (f32[96]{0:T(128)S(1)}, f32[96]{0:T(128)}, u32[]{:S(2)}) copy-start(f32[96]{0:T(128)} %dynamic_slice.23) | copy-start | bytes 1156
  98.1 5.5 %copy-start.7 = (bf16[64,256]{1,0:T(8,128)(2,1)S(1)}, bf16[64,256]{1,0:T(8,128)(2,1)}, u32[]{:S(2)}) copy-start(bf16[64,256]{1,0:T(8,128)(2,1)} %param.30) | copy-start | bytes 98308
  98.1 5.5 %copy-start.11 = (f32[64]{0:T(128)S(1)}, f32[64]{0:T(128)}, u32[]{:S(2)}) copy-start(f32[64]{0:T(128)} %param.26) | copy-start | bytes 772
  98.1 32.8 %all-to-all-start.1 = ((f32[2,96,24,128]{3,2,1,0:T(8,128)}), f32[2,96,24,128]{3,2,1,0:T(8,128)}, u32[]{:S(2)}, u32[]{:S(2)}) async-start(f32[2,96,24,128]{3,2,1,0:T(8,128)} %broadcast_in_dim.11), calls=%async_computation.1 | async-start | bytes 4718592 | tf_op jit(solution)/shard_map/all_to_all | solution.py:11
  103.5 6.5 %copy-start.8 = (bf16[64,256]{1,0:T(8,128)(2,1)S(1)}, bf16[64,256]{1,0:T(8,128)(2,1)}, u32[]{:S(2)}) copy-start(bf16[64,256]{1,0:T(8,128)(2,1)} %param.29) | copy-start | bytes 98308
  113.9 20.0 %copy-start.4 = (bf16[96,24,128]{2,1,0:T(8,128)(2,1)S(1)}, bf16[96,24,128]{2,1,0:T(8,128)(2,1)}, u32[]{:S(2)}) copy-start(bf16[96,24,128]{2,1,0:T(8,128)(2,1)} %param.21) | copy-start | bytes 1769476
  113.9 20.0 %copy-start.15 = (f32[128]{0:T(128)S(1)}, f32[128]{0:T(128)}, u32[]{:S(2)}) copy-start(f32[128]{0:T(128)} %param.25) | copy-start | bytes 1540
  135.6 15.6 %copy-start.6 = (bf16[128,640]{1,0:T(8,128)(2,1)S(1)}, bf16[128,640]{1,0:T(8,128)(2,1)}, u32[]{:S(2)}) copy-start(bf16[128,640]{1,0:T(8,128)(2,1)} %param.33) | copy-start | bytes 491524
  135.6 15.6 %copy-start.18 = (f32[128]{0:T(128)S(1)}, f32[128]{0:T(128)}, u32[]{:S(2)}) copy-start(f32[128]{0:T(128)} %param.32) | copy-start | bytes 1540
  142.7 14.5 %copy-start.3 = (f32[96,24,8]{1,2,0:T(8,128)}, f32[96,24,8]{1,2,0:T(8,128)S(1)}, u32[]{:S(2)}) copy-start(f32[96,24,8]{1,2,0:T(8,128)S(1)} %get-tuple-element.13) | copy-start | bytes 221188
  143.5 13.6 %all-to-all-start.2 = ((f32[16,96,8]{1,2,0:T(8,128)}), f32[16,96,8]{1,2,0:T(8,128)S(1)}, u32[]{:S(2)}, u32[]{:S(2)}) async-start(f32[16,96,8]{1,2,0:T(8,128)} %broadcast_in_dim.12), calls=%async_computation.2 | async-start | bytes 131072 | tf_op jit(solution)/shard_map/all_to_all | solution.py:11
  158.2 11.3 %all-to-all-start.3 = ((f32[16,96,8]{1,2,0:T(8,128)}), f32[16,96,8]{1,2,0:T(8,128)S(1)}, u32[]{:S(2)}, u32[]{:S(2)}) async-start(f32[16,96,8]{1,2,0:T(8,128)} %broadcast_in_dim.13), calls=%async_computation.3 | async-start | bytes 131072 | tf_op jit(solution)/shard_map/all_to_all | solution.py:11
  169.5 25.6 %all-to-all-start.5 = ((bf16[128,12,2,96]{3,2,1,0:T(2,128)(2,1)}), bf16[128,12,2,96]{3,2,1,0:T(2,128)(2,1)S(1)}, u32[]{:S(2)}, u32[]{:S(2)}) async-start(bf16[128,12,2,96]{3,2,1,0:T(2,128)(2,1)} %copy.136), calls=%async_computation.5 | async-start | bytes 1572864 | tf_op jit(solution)/shard_map/all_to_all | solution.py:171
  197.9 10.8 %copy-start.19 = (bf16[256,64]{0,1:T(8,128)(2,1)S(1)}, bf16[256,64]{0,1:T(8,128)(2,1)}, u32[]{:S(2)}) copy-start(bf16[256,64]{0,1:T(8,128)(2,1)} %param.31) | copy-start | bytes 98308
  198.9 26.0 %all-to-all-start.6 = ((bf16[128,96,24]{1,2,0:T(8,128)(2,1)}), bf16[128,96,24]{1,2,0:T(8,128)(2,1)S(1)}, u32[]{:S(2)}, u32[]{:S(2)}) async-start(bf16[128,96,24]{1,2,0:T(8,128)(2,1)} %bitcast.35), calls=%async_computation.6 | async-start | bytes 1572864 | tf_op jit(solution)/shard_map/all_to_all | solution.py:180
  224.9 26.9 %all-to-all-start.4 = ((bf16[16,128,6,64]{1,3,2,0:T(8,128)(2,1)}), bf16[16,128,6,64]{1,3,2,0:T(8,128)(2,1)S(1)}, u32[]{:S(2)}, u32[]{:S(2)}) async-start(bf16[16,128,6,64]{1,3,2,0:T(8,128)(2,1)} %bitcast.113), calls=%async_computation.4 | async-start | bytes 3145728 | tf_op jit(solution)/shard_map/all_to_all | solution.py:47
  234.1 18.7 %copy-start.1 = (bf16[1024,128]{1,0:T(8,128)(2,1)S(1)}, bf16[1024,128]{1,0:T(8,128)(2,1)}, u32[]{:S(2)}) copy-start(bf16[1024,128]{1,0:T(8,128)(2,1)} %param.24) | copy-start | bytes 786436
  236.7 15.4 %copy-start.5 = (bf16[128,6,64]{0,2,1:T(8,128)(2,1)S(1)}, bf16[128,6,64]{0,2,1:T(8,128)(2,1)}, u32[]{:S(2)}) copy-start(bf16[128,6,64]{0,2,1:T(8,128)(2,1)} %param.18) | copy-start | bytes 294916
  (7 other events, 14.3 us)
Sparse Core Ops, SparseCore 0:
  39.2 30.1 all-gather.2

commit v2 on v0

v2 whole, which is shorter than its diff:
```python
import functools

import jax
import jax.numpy as jnp
from jax import lax
from jax.experimental import pallas as pl
from jax.experimental.pallas import tpu as pltpu
from jax.sharding import PartitionSpec as P

MESH = pl.DeviceIdType.MESH
EPS = 1e-05
F32 = jnp.float32
BF16 = jnp.bfloat16
NR, NC, ND = 4, 16, 2
ALL = NR * NC * ND
TOK, PAD = 6, 8
COLS = 24


def nt(a, b):
    return lax.dot_general(a, b, (((1,), (1,)), ((), ())), preferred_element_type=F32)


def nn(a, b):
    return lax.dot_general(a, b, (((1,), (0,)), ((), ())), preferred_element_type=F32)


def tn(a, b):
    return lax.dot_general(a, b, (((0,), (0,)), ((), ())), preferred_element_type=F32)


def sigmoid(x):
    return 1.0 / (1.0 + jnp.exp(-x))


def split2(x):
    hi = x.astype(BF16)
    return hi, (x - hi.astype(F32)).astype(BF16)


def normed_rows(x):
    centred = x - jnp.mean(x, axis=0, keepdims=True)
    variance = jnp.mean(centred * centred, axis=0, keepdims=True)
    return centred * lax.rsqrt(variance + EPS)


def iota(rows, columns, dim):
    return lax.broadcasted_iota(jnp.int32, (rows, columns), dim)


def column_of(row, n):
    return jnp.broadcast_to(row, (n, row.shape[1])).T


def landed(ref, sem):
    pltpu.make_async_copy(ref, ref, sem).wait()


def kernel(
    x_tok, x_blk, couple, present, genuine, opm_gain, entry, final, offset_row, score_gain, score,
    tri_gain_row, tri, res_gain_row, res, seq_gain_row, content, gate_w, out_w,
    revised, pair_out,
    l_f32, l_msg, r_msg, l_buf, r_buf, outer, pair, gate4, tri_f32, tri_msg, tri_buf,
    logit, p_msg, st_msg, p_buf, st_buf, x_buf, xn_buf, v_buf, d_msg, d_buf,
    tl_all, tr_all, z_msg, z_buf, z_f32,
    ri_mask, cj_flag, final_t, offset, score_t, tri_gain, tri_t, res_gain, res_t,
    val_bd, gate_bd, out_bd,
    send, recv, plane_sem,
):
    r = lax.axis_index("row")
    c = lax.axis_index("col")
    d = lax.axis_index("depth")
    me = r * (NC * ND) + c * ND + d
    own = lax.rem(c, 8)
    half = c // 8
    core = lax.rem(c, 2)
    sibling = (r, c + 1 - 2 * core, d)

    def remote(src, dst, k, dev):
        pltpu.make_async_remote_copy(
            src, dst, send.at[k], recv.at[k], device_id=dev, device_id_type=MESH
        ).start()

    def local(src, dst, k):
        pltpu.make_async_copy(src, dst, recv.at[k]).start()

    def finish(k):
        if k >= 2:
            landed(l_buf.at[pl.ds(0, 7)], send.at[0])
            landed(l_buf.at[pl.ds(0, 8)], send.at[9])
            for _ in range(NR * ND - 1):
                landed(r_msg, send.at[1])
            landed(x_buf.at[0, pl.ds(0, 31)], send.at[2])
        if k >= 5:
            landed(tri_msg.at[pl.ds(0, ALL - 1)], send.at[3])
            landed(p_buf.at[pl.ds(0, NC - 1)], send.at[4])
            landed(st_buf.at[pl.ds(0, NC - 1)], send.at[5])
            landed(x_buf.at[0], send.at[10])

            @pl.when(core != d)
            def _():
                landed(p_msg, send.at[4])
                landed(st_msg, send.at[5])
        if k >= 8:
            landed(d_buf.at[pl.ds(0, 7)], send.at[6])
            landed(z_buf.at[pl.ds(0, ALL - 1)], send.at[7])

            @pl.when(half != core)
            def _():
                landed(d_msg.at[0], send.at[6])
        if k >= 2:
            @pl.when(half != d)
            def _():
                landed(l_msg, send.at[0])

            @pl.when((r * 4 + c // 4) != c)
            def _():
                landed(r_msg, send.at[1])
        if k >= 9:
            landed(pair_out.at[d], send.at[8])
            landed(pair_out.at[1 - d], recv.at[8])

    def prepare():
        flags = genuine[...].astype(F32)
        lane = iota(128, 128, 1)
        token = r * 96 + d * 48 + (lane // 16) * TOK + lax.rem(lane, PAD)
        valid = lax.rem(lane, PAD) < TOK
        ri = jnp.zeros((8, 128), F32)
        cj = jnp.zeros((COLS, 128), F32)
        for k in range(3):
            row = flags[k : k + 1].astype(BF16)
            pick = jnp.logical_and(iota(128, 128, 0) + k * 128 == token, valid)
            ri += nn(jnp.broadcast_to(row, (8, 128)), pick.astype(BF16))
            mine = iota(COLS, 128, 1) + k * 128 == c * COLS + iota(COLS, 128, 0)
            cj += nt(mine.astype(BF16), jnp.broadcast_to(row, (128, 128)))
        ri_mask[...] = ri
        cj_flag[...] = cj
        for k in range(2):
            part = final[:, k].reshape(512, 128).astype(F32)
            final_t[k * 128 : (k + 1) * 128, :] = part.T.astype(BF16)
        offset[...] = column_of(offset_row[...], 128)
        tri_gain[...] = column_of(tri_gain_row[...], 128)
        res_gain[...] = column_of(res_gain_row[...], 128)
        score_t[...] = score[...].T * score_gain[...]
        tri_t[...] = tri[...].astype(F32).T.astype(BF16)
        res_t[...] = res[...].astype(F32).T.astype(BF16)
        row, col = iota(256, 256, 0), iota(256, 256, 1)
        same = row // 64 == lax.rem(col // 32, 4)
        same_t = lax.rem(row // 32, 4) == col // 64
        spread = (iota(64, 256, 0) == lax.rem(iota(64, 256, 1), 64)).astype(BF16)
        out4 = nn(out_w[...], spread).astype(BF16)
        for hp in range(4):
            pick = (row == (2 * hp + col // 128) * 32 + lax.rem(col, 32)).astype(BF16)
            for w, out in ((content, val_bd), (gate_w, gate_bd)):
                rows4 = jnp.concatenate([nn(w[...], pick)] * 4, axis=0)
                out[hp] = jnp.where(same, rows4, 0.0).astype(BF16)
            pick_t = (col == (2 * hp + row // 128) * 32 + lax.rem(row, 32)).astype(BF16)
            out_bd[hp] = jnp.where(same_t, nn(pick_t, out4), 0.0).astype(BF16)

    barrier = pltpu.get_barrier_semaphore()

    def greet(k, _):
        p = lax.rem(c * ND + d + k, NC * ND)
        pl.semaphore_signal(barrier, inc=1, device_id=(r, p // 2, lax.rem(p, 2)), device_id_type=MESH)
        return 0

    lax.fori_loop(1, NC * ND, greet, 0)
    for k in range(1, NR):
        pl.semaphore_signal(barrier, inc=1, device_id=(lax.rem(r + k, NR), c, d), device_id_type=MESH)

    l_f32[...] = jnp.zeros_like(l_f32)
    here = present[...].astype(F32)
    s_mask = jnp.where(d == 0, here[0:1], here[1:2])
    inv_count = 1.0 / (jnp.sum(here, keepdims=True).reshape(1, 1) + 0.001)
    gain0 = column_of(opm_gain[...], 128)
    entry_t = entry[...].astype(F32).T.astype(BF16)
    for t in range(TOK):
        x = normed_rows(x_tok[t].astype(F32)) * gain0
        f = nn(entry_t, x.astype(BF16)) * s_mask
        l_f32[pl.ds(t, 32, stride=PAD), :] = f[:32]
        r_msg[t * 32 : (t + 1) * 32, :] = f[32:].astype(BF16)
    l_msg[...] = l_f32[...].reshape(16, 16, 128).astype(BF16)

    pl.semaphore_wait(barrier, NC * ND - 1 + NR - 1)
    for k in range(1, NR):
        pl.semaphore_signal(plane_sem, inc=1, device_id=(lax.rem(r + k, NR), c, d), device_id_type=MESH)

    lane_half = pl.ds(pl.multiple_of(d * 128, 128), 128)
    l_dst = l_buf.at[:, pl.ds(pl.multiple_of(own * 16, 16), 16), lane_half]
    self_l = half == d

    @pl.when(self_l)
    def _():
        local(l_msg, l_dst, 0)

    @pl.when(jnp.logical_not(self_l))
    def _():
        remote(l_msg, l_dst, 0, (r, c, half))

    def send_l(k, _):
        remote(l_msg, l_dst, 0, (r, lax.rem(c + 2 * k, NC), half))
        return 0

    lax.fori_loop(1, 8, send_l, 0)

    pl.semaphore_wait(plane_sem, NR - 1)

    c_t = r * 4 + c // 4
    r_dst = r_buf.at[pl.ds(pl.multiple_of(lax.rem(c, 4) * 192, 192), 192), lane_half]
    self_r = c_t == c

    @pl.when(self_r)
    def _():
        local(r_msg, r_dst, 1)

    @pl.when(jnp.logical_not(self_r))
    def _():
        remote(r_msg, r_dst, 1, (r, c_t, d))

    def send_r(k, _):
        remote(r_msg, r_dst, 1, (lax.rem(r + k // 2, NR), c_t, lax.rem(d + k, ND)))
        return 0

    lax.fori_loop(1, NR * ND, send_r, 0)

    prepare()

    landed(l_buf.at[pl.ds(0, 8)], recv.at[0])
    for k in range(4):
        block = l_buf.at[:, pl.ds(pl.multiple_of((2 * k + core) * 16, 16), 16), :]
        remote(block, block, 9, sibling)

    x_dst = x_buf.at[core, r * 8 + c // 2]
    local(x_blk.at[c // 2], x_dst, 2)

    def send_x(k, _):
        b = lax.rem(c // 2 + k // 4, 8)
        remote(x_blk.at[b], x_dst, 2, (lax.rem(r + k, NR), 2 * b + core, d))
        return 0

    lax.fori_loop(1, 32, send_x, 0)

    landed(r_buf, recv.at[1])
    landed(l_buf.at[pl.ds(0, 8)], recv.at[9])

    def outer_step(k, _):
        outer[k] = nt(r_buf[...], l_buf[k]).astype(BF16)
        return 0

    lax.fori_loop(0, 16, outer_step, 0)

    lane = lax.broadcasted_iota(jnp.int32, (128, 128), 1)
    first = lax.rem(lane // PAD, 2) == 0
    first4 = first[:4]
    is_left = lax.rem(lane // PAD, 2) == d
    logit[...] = jnp.full(logit.shape, -3e38, F32)
    score_hi, score_lo = split2(score_t[...])
    ri = ri_mask[0:1, :]
    score_both = jnp.concatenate([score_hi, score_lo], axis=0)

    def column(j, _):
        rhs = outer[:, pl.ds(pl.multiple_of(j * 32, 32), 32), :].reshape(512, 128)
        o = nn(final_t[...], rhs)
        t = jnp.where(first, o[:128], o[128:])
        u = t + jnp.where(first, pltpu.roll(t, 120, 1), pltpu.roll(t, 8, 1))
        one = (couple[j].astype(F32) + (u * inv_count + offset[...])).astype(BF16)
        pair[j] = one
        x = normed_rows(one.astype(F32))
        x_hi, x_lo = split2(x)
        two = nn(score_both, x_hi)
        flag = cj_flag[pl.ds(j, 1), :]
        lg = two[:8] + two[8:] + nn(score_hi, x_lo) + 1e9 * (flag - 1.0)
        m = j // TOK
        row = lax.rem(m, 2) * 16 + (m // 2) * PAD + lax.rem(j, TOK)
        logit[pl.ds(row, 4, stride=32), :] = jnp.where(first4, lg[:4], lg[4:])
        q = nn(tri_t[...], (x * tri_gain[...]).astype(BF16))
        sg = sigmoid(jnp.where(is_left, q[0:128], q[256:384]))
        tri = sg * jnp.where(is_left, q[128:256], q[384:512]) * (flag * ri)
        tri_f32[pl.ds(j, 128, stride=COLS), :] = tri
        gate4[j] = sigmoid(q[512:640])
        return 0

    lax.fori_loop(0, COLS, column, 0)

    tri_msg[...] = tri_f32[...].reshape(128, COLS, 128).astype(BF16)
    local(tri_msg.at[me], tri_buf.at[r, c, d], 3)

    def send_t(k, _):
        p = lax.rem(me + k, ALL)
        remote(tri_msg.at[p], tri_buf.at[r, c, d], 3, (p // 32, lax.rem(p // 2, NC), lax.rem(p, ND)))
        return 0

    lax.fori_loop(1, ALL, send_t, 0)

    lg = logit[...].reshape(4, 32, 128)
    top = jnp.max(lg, axis=1, keepdims=True)
    e = jnp.exp(lg - top)
    p_msg[...] = e.astype(BF16)
    st_msg[...] = jnp.concatenate([top[:, 0], jnp.sum(e, axis=1)], axis=0)
    self_p = core == d

    @pl.when(self_p)
    def _():
        local(p_msg, p_buf.at[c], 4)
        local(st_msg, st_buf.at[c], 5)

    @pl.when(jnp.logical_not(self_p))
    def _():
        dev = (r, c - core + d, d)
        remote(p_msg, p_buf.at[c], 4, dev)
        remote(st_msg, st_buf.at[c], 5, dev)

    def send_p(k, _):
        dev = (r, 2 * lax.rem(c // 2 + k // 2, 8) + d, lax.rem(d + k, ND))
        remote(p_msg, p_buf.at[c], 4, dev)
        remote(st_msg, st_buf.at[c], 5, dev)
        return 0

    lax.fori_loop(1, NC, send_p, 0)

    landed(x_buf.at[core], recv.at[2])
    remote(x_buf.at[core], x_buf.at[core], 10, sibling)

    landed(tri_buf, recv.at[3])
    first384 = lax.rem(lax.broadcasted_iota(jnp.int32, (384, 128), 1) // PAD, 2) == 0
    for k in range(NR):
        t0 = tri_buf[k, :, 0].astype(F32).reshape(384, 128)
        t1 = tri_buf[k, :, 1].astype(F32).reshape(384, 128)
        tl_all[:, k * 128 : (k + 1) * 128] = jnp.where(first384, t0, t1).astype(BF16)
        tr_all[:, k * 128 : (k + 1) * 128] = jnp.where(first384, t1, t0).astype(BF16)
    for k in range(NR):
        z = tn(tr_all[:, k * 128 : (k + 1) * 128], tl_all[...])
        for i in range(NR):
            zi = z[:, i * 128 : (i + 1) * 128]
            up, down = pltpu.roll(zi, 8, 1), pltpu.roll(zi, 120, 1)
            zi, up, down = (a.reshape(2, 2, 2, 2, PAD, 128) for a in (zi, up, down))
            mask = first[:8]
            keep = jnp.where(mask, zi[:, 0], up[:, 1])
            other = jnp.where(mask, down[:, 0], zi[:, 1])
            for hi in range(2):
                for lo in range(2):
                    to = k * 4 + hi * 2 + lo
                    z_msg[i, to, 0] = keep[lo, :, 1 - hi].reshape(16, 128).astype(BF16)
                    z_msg[i, to, 1] = other[lo, :, 1 - hi].reshape(16, 128).astype(BF16)
    local(z_msg.at[r, c, d], z_buf.at[me], 7)

    def send_z(k, _):
        p = lax.rem(me + k, ALL)
        dev = (p // 32, lax.rem(p // 2, NC), lax.rem(p, ND))
        remote(z_msg.at[dev[0], dev[1], dev[2]], z_buf.at[me], 7, dev)
        return 0

    lax.fori_loop(1, ALL, send_z, 0)

    landed(x_buf.at[1 - core], recv.at[10])
    landed(p_buf, recv.at[4])
    landed(st_buf, recv.at[5])
    ones_bd = (iota(256, 256, 0) // 64 == iota(256, 256, 1) // 64).astype(BF16)
    seq_gain = jnp.concatenate([seq_gain_row[...]] * 4, axis=1)
    for g in range(4):
        lanes = slice(g * 256, (g + 1) * 256)
        x = x_buf[:, :, :, lanes].astype(F32).reshape(512, 256)
        mean = nn(x.astype(BF16), ones_bd) * (1.0 / 64)
        centred = x - mean
        s_hi, s_lo = split2(centred * centred)
        variance = (nn(s_hi, ones_bd) + nn(s_lo, ones_bd)) * (1.0 / 64)
        xn = (centred * lax.rsqrt(variance + EPS) * seq_gain).astype(BF16)
        xn_buf[:, lanes] = xn
        for hp in range(4):
            v = nn(xn, val_bd[hp]).astype(BF16)
            v_buf[2 * hp, :, g * 128 : (g + 1) * 128] = v[:, :128]
            v_buf[2 * hp + 1, :, g * 128 : (g + 1) * 128] = v[:, 128:]

    tops = st_buf[:, 0:4, :]
    factor = jnp.exp(tops - jnp.max(tops, axis=0, keepdims=True))
    total = jnp.sum(factor * st_buf[:, 4:8, :], axis=0, keepdims=True)
    factor = factor / total
    averaged = [None] * 8
    for h in range(4):
        w = p_buf[:, h].astype(F32) * factor[:, h : h + 1, :]
        w = jnp.concatenate([w[:, :16].reshape(256, 128), w[:, 16:].reshape(256, 128)], axis=0).astype(BF16)
        for b in range(2):
            a = tn(w, v_buf[h + 4 * b]).reshape(4, 2, 2, PAD, 512)
            averaged[h + 4 * b] = jnp.concatenate([a[:, k, b].reshape(32, 512) for k in range(2)], axis=0)
    base = pl.multiple_of(r * 64 + core * 32, 32)
    for g in range(4):
        lanes = slice(g * 256, (g + 1) * 256)
        xi = jnp.concatenate([xn_buf[pl.ds(base + 256 * k, 32), lanes] for k in range(2)], axis=0)
        acc = jnp.zeros((64, 256), F32)
        for hp in range(4):
            gates = sigmoid(nn(xi, gate_bd[hp]))
            a = jnp.concatenate(
                [averaged[2 * hp + b][:, g * 128 : (g + 1) * 128] for b in range(2)], axis=1
            )
            hi, lo = split2(gates * a)
            acc += nn(hi, out_bd[hp]) + nn(lo, out_bd[hp])
        d_msg[:, :, lanes] = acc.reshape(8, PAD, 256).astype(BF16)

    self_d = half == core
    d_dst = d_buf.at[c // 2]
    d_first = d_msg.at[lax.rem(own, 2) * 4 + own // 2]

    @pl.when(self_d)
    def _():
        local(d_first, d_dst, 6)

    @pl.when(jnp.logical_not(self_d))
    def _():
        remote(d_first, d_dst, 6, (r, core * 8 + own, d))

    def send_d(k, _):
        o = lax.rem(own + k, 8)
        remote(d_msg.at[lax.rem(o, 2) * 4 + o // 2], d_dst, 6, (r, core * 8 + o, d))
        return 0

    lax.fori_loop(1, 8, send_d, 0)

    landed(z_buf, recv.at[7])
    z = z_buf[...].astype(F32)
    z_f32[...] = normed_rows(z).reshape(2048, 128)
    for m in range(2):
        for t in range(TOK):
            zq = z_f32[pl.ds(m * PAD + t, 128, stride=16), :] * res_gain[...]
            f = nn(res_t[...], zq.astype(BF16))
            j0, j1 = m * TOK + t, (2 + m) * TOK + t
            one = jnp.where(first, pair[j0].astype(F32), pair[j1].astype(F32))
            g4 = jnp.where(first, gate4[j0], gate4[j1])
            pair_out[d, m * TOK + t] = (one + g4 * f).T.astype(BF16)
    remote(pair_out.at[d], pair_out.at[d], 8, (r, c, 1 - d))

    landed(d_buf, recv.at[6])
    revised[...] = (x_blk[...].astype(F32) + d_buf[...].astype(F32)).astype(BF16)


    finish(9)


def on_device(
    sequence_stack, present_sequence_flags, genuine_residue_flags, couple_state,
    tensor_scale, tensor_entry_matrix, tensor_final_matrix, tensor_offset,
    mean_sequence_scale, mean_couple_scale, mean_score_matrix, mean_content_matrix,
    mean_sigmoid_matrix, mean_final_matrix, trimul_scale, trimul_entry_matrix,
    trimul_result_scale, trimul_final_matrix,
):
    d = lax.axis_index("depth")
    x_tok = jnp.transpose(sequence_stack, (1, 2, 0))
    x_blk = jnp.transpose(sequence_stack.reshape(8, 16, TOK, 64), (0, 2, 1, 3)).reshape(8, TOK, 1024)
    x_blk = jnp.pad(x_blk, ((0, 0), (0, PAD - TOK), (0, 0)))
    lane = jnp.arange(128)
    place = jnp.where(lane % PAD < TOK, (lane // 16) * TOK + lane % PAD, -1)
    spread = (jnp.arange(48)[:, None] == place[None, :]).astype(BF16)
    mine = lax.dynamic_slice_in_dim(couple_state, d * 48, 48, 0)
    couple = jnp.einsum("ijc,ip->jcp", mine, spread, preferred_element_type=F32).astype(BF16)
    vm = pl.BlockSpec(memory_space=pltpu.VMEM)
    row = lambda v: v.reshape(1, -1)
    args = (
        x_tok, x_blk, couple, present_sequence_flags.reshape(2, 128), genuine_residue_flags.reshape(3, 128),
        row(tensor_scale), tensor_entry_matrix, tensor_final_matrix.reshape(16, 2, 32, 128), row(tensor_offset),
        row(mean_couple_scale), mean_score_matrix, row(trimul_scale), trimul_entry_matrix,
        row(trimul_result_scale), trimul_final_matrix, row(mean_sequence_scale),
        mean_content_matrix, mean_sigmoid_matrix, mean_final_matrix,
    )
    V = pltpu.VMEM
    revised, pair_out = pl.pallas_call(
        kernel,
        name="msa_block",
        out_shape=(
            jax.ShapeDtypeStruct((8, PAD, 1024), BF16),
            jax.ShapeDtypeStruct((2, 12, 128, 128), BF16),
        ),
        in_specs=[vm] * len(args),
        out_specs=(vm, vm),
        scratch_shapes=[
            V((256, 128), F32), V((16, 16, 128), BF16), V((192, 128), BF16),
            V((16, 128, 256), BF16), V((768, 256), BF16), V((16, 768, 128), BF16),
            V((COLS, 128, 128), BF16), V((COLS, 128, 128), F32),
            V((128 * COLS, 128), F32), V((128, COLS, 128), BF16), V((NR, NC, ND, COLS, 128), BF16),
            V((128, 128), F32), V((4, 32, 128), BF16), V((8, 128), F32),
            V((NC, 4, 32, 128), BF16), V((NC, 8, 128), F32),
            V((2, 32, PAD, 1024), BF16), V((512, 1024), BF16), V((8, 512, 512), BF16),
            V((8, PAD, 1024), BF16), V((8, PAD, 1024), BF16),
            V((384, 512), BF16), V((384, 512), BF16),
            V((NR, NC, ND, 16, 128), BF16), V((128, 16, 128), BF16), V((2048, 128), F32),
            V((8, 128), F32), V((COLS, 128), F32), V((256, 512), BF16), V((128, 128), F32), V((8, 128), F32),
            V((128, 128), F32), V((640, 128), BF16), V((128, 128), F32), V((128, 128), BF16),
            V((4, 256, 256), BF16), V((4, 256, 256), BF16), V((4, 256, 256), BF16),
            pltpu.SemaphoreType.DMA((11,)), pltpu.SemaphoreType.DMA((11,)),
            pltpu.SemaphoreType.REGULAR,
        ],
        compiler_params=pltpu.CompilerParams(
            collective_id=0, has_side_effects=True, vmem_limit_bytes=56 * 1024 * 1024
        ),
    )(*args)
    revised = revised[:, :TOK].reshape(8, TOK, 16, 64)
    revised = jnp.transpose(revised, (0, 2, 1, 3)).reshape(128, TOK, 64)
    pair_out = pair_out.reshape(2, 2, TOK, 8, 2, PAD, 128)[:, :, :, :, :, :TOK]
    pair_out = jnp.transpose(pair_out, (0, 3, 5, 4, 1, 2, 6)).reshape(96, COLS, 128)
    return revised, pair_out


def solution(mesh):
    placed = (P("depth", ("row", "col"), None), P(), P(), P("row", "col", None)) + (P(),) * 14
    return jax.shard_map(
        on_device,
        mesh=mesh,
        in_specs=placed,
        out_specs=(P("depth", ("row", "col"), None), P("row", "col", None)),
        check_vma=False,
    )
```

time: 342 us -> 103 us (0.30)
  waiting for transfers between devices: 126 us -> 0 us
  Pallas kernels: 0 us -> 91.5 us
  matrix products: 69.8 us -> 1.3 us
  local copies, waits for them, and re-layouts: 50.8 us -> 9.45 us
  starting transfers between devices: 31.1 us -> 0 us
  blocking collectives: 28.6 us -> 0 us
  other arithmetic: 18.7 us -> 0.01 us
  between operations: 15.1 us -> 0.69 us
    pallas_call x0 -> x1, Pallas kernels: none -> 91.5 us  [on_device(): pl.pallas_call(kernel, name='msa_block', out_shape=(jax.ShapeDtypeStruct(...]
    all_to_all x5 -> x0, waiting for transfers between devices: 73.8 us -> none  [sent_to_all(): lax.all_to_all(jnp.broadcast_to(array[None], (size, *array.shape)), axis,...]
    dot_general x11 -> x1, matrix products: 69.8 us -> 1.3 us  [on_device(): jnp.einsum('ijc,ip->jcp', mine, spread, preferred_element_type=F32)]
    all_to_all x5 -> x0, starting transfers between devices: 31 us -> none  [sent_to_all(): lax.all_to_all(jnp.broadcast_to(array[None], (size, *array.shape)), axis,...]
    all_to_all x1 -> x0, blocking collectives: 28.6 us -> none  [sum_at_owner(): tiles = lax.all_to_all(split_up(array, dim, size), axis, 0, 0, tiled=True)]
    all_gather x1 -> x0, waiting for transfers between devices: 28.2 us -> none  [broadcast(): lax.all_gather(array, axis)]
    reduce_scatter x1 -> x0, waiting for transfers between devices: 24.2 us -> none  [on_device(): lax.psum_scatter(partial_product.astype(jnp.bfloat16), 'col', scatter_dim...]
    reshape x3 -> x4, local copies, waits for them, and re-layouts: 19.6 us -> 1.43 us  [the longest x1 1.02 us: on_device(): jnp.transpose(pair_out, (0, 3, 5, 4, 1, 2, 6)).reshape(96, COLS, 128)]
  transfers between devices with their start and end apart: 7 -> 0, of which waited for: 6 -> 0; matrix products, arithmetic and copies ran while one was open for 18% -> 0% of each run, Pallas kernels for 0% -> 0%
where the time goes in v2:
time: 103 us
  Pallas kernels  91.5 us (89%)
  local copies, waits for them, and re-layouts  9.45 us (9%)
  matrix products  1.3 us (1%)
    pallas_call x1, Pallas kernels, on_device(): pl.pallas_call(kernel, name='msa_block', out_shape=(jax.ShapeDtypeStruct(...  91.5 us
    unnamed x7, local copies, waits for them, and re-layouts  6.34 us

profile of v2, /device:TPU:1, one launch (start us, length us, event | category | flops | bytes accessed | tf_op | source)
XLA Modules:
  0.0 103.0 jit_solution(693056876926066578)
XLA Ops:
  0.6 0.0 copy-start
  0.7 1.5 %copy.29.score = f32[128,8]{1,0:T(8,128)} copy(f32[128,8]{0,1:T(8,128)} %param.28) | data formatting | bytes 8192 | tf_op args[10]
  2.1 1.5 %copy.30.out_w = bf16[256,64]{1,0:T(8,128)(2,1)} copy(bf16[256,64]{0,1:T(8,128)(2,1)} %param.31) | data formatting | bytes 65536 | tf_op args[13]
  3.6 1.1 %copy.26 = bf16[128,6,64]{2,0,1:T(8,128)(2,1)S(1)} copy(bf16[128,6,64]{0,2,1:T(8,128)(2,1)} %param.18) | data formatting | bytes 196608 | tf_op args[0]
  4.7 0.2 reshape.74
  4.9 0.1 copy.27
  4.9 0.7 pad.4.x_blk
  5.6 0.0 copy-done
  5.6 1.3 %convolution_convert_fusion.couple = bf16[24,128,128]{2,1,0:T(8,128)(2,1)} fusion(bf16[48,24,128]{2,1,0:T(8,128)(2,1)S(1)} %constant_dynamic-slice_fusion, s32[128]{0:T(128)S(1)} %compare_select_fusion), kind=kOutput, calls=%fused_computation | convolution fusion | flops 38148096 | bytes 1081856 | tf_op jit(solution)/shard_map/ijc,ip->jcp/dot_general | solution.py:453
  6.9 91.5 %msa_block.1 = (bf16[8,8,1024]{2,1,0:T(8,128)(2,1)}, bf16[2,12,128,128]{3,2,1,0:T(8,128)(2,1)}) custom-call(bf16[6,64,128]{2,1,0:T(8,128)(2,1)} %bitcast.35, bf16[8,8,1024]{2,1,0:T(8,128)(2,1)} %pad.4.x_blk, bf16[24,128,128]{2,1,0:T(8,128)(2,1)} %convolution_convert_fusion.couple, s32[2,128]{1,0:T(2,128)} %bitcast.39, s32[3,128]{1,0:T(4,128)} %bitcast.38, ...), custom_call_target="tpu_custom_call" | custom-call | tf_op jit(solution)/shard_map/msa_block/pallas_call | solution.py:464
  98.5 1.0 copy.31
  99.5 1.5 %copy.39 = bf16[2,2,6,8,2,6,128]{6,2,1,4,5,3,0:T(8,128)(2,1)S(1)} copy(bf16[2,2,6,8,2,6,128]{6,5,4,3,2,1,0:T(8,128)(2,1)} %bitcast.32) | data formatting | bytes 1179648
  101.0 1.0 reshape.87
  102.0 0.2 reshape.84
  102.2 0.8 copy.33
  (2 shorter events, 0.0 us)
Async XLA Ops:
  0.6 5.0 %copy-start = (bf16[96,24,128]{2,1,0:T(8,128)(2,1)S(1)}, bf16[96,24,128]{2,1,0:T(8,128)(2,1)}, u32[]{:S(2)}) copy-start(bf16[96,24,128]{2,1,0:T(8,128)(2,1)} %param.21) | copy-start | bytes 1769476

commit v3 on v2

--- a/solution.py
+++ b/solution.py
@@ -6,6 +6,7 @@
 from jax.experimental import pallas as pl
 from jax.experimental.pallas import tpu as pltpu
 from jax.sharding import PartitionSpec as P
+
 
 MESH = pl.DeviceIdType.MESH
 EPS = 1e-05
@@ -15,6 +16,7 @@
 ALL = NR * NC * ND
 TOK, PAD = 6, 8
 COLS = 24
+GROUP = 6
 
 
 def nt(a, b):
@@ -64,7 +66,7 @@
     logit, p_msg, st_msg, p_buf, st_buf, x_buf, xn_buf, v_buf, d_msg, d_buf,
     tl_all, tr_all, z_msg, z_buf, z_f32,
     ri_mask, cj_flag, final_t, offset, score_t, tri_gain, tri_t, res_gain, res_t,
-    val_bd, gate_bd, out_bd,
+    val_bd, gate_bd, out_bd, out_f32,
     send, recv, plane_sem,
 ):
     r = lax.axis_index("row")
@@ -88,8 +90,7 @@
         if k >= 2:
             landed(l_buf.at[pl.ds(0, 7)], send.at[0])
             landed(l_buf.at[pl.ds(0, 8)], send.at[9])
-            for _ in range(NR * ND - 1):
-                landed(r_msg, send.at[1])
+            landed(r_buf.at[pl.ds(0, 672)], send.at[11])
             landed(x_buf.at[0, pl.ds(0, 31)], send.at[2])
         if k >= 5:
             landed(tri_msg.at[pl.ds(0, ALL - 1)], send.at[3])
@@ -113,12 +114,12 @@
             def _():
                 landed(l_msg, send.at[0])
 
-            @pl.when((r * 4 + c // 4) != c)
+            @pl.when(jnp.logical_not(jnp.logical_and(r * 4 + c // 4 == c, lax.rem(c, 4) == r)))
             def _():
                 landed(r_msg, send.at[1])
         if k >= 9:
-            landed(pair_out.at[d], send.at[8])
-            landed(pair_out.at[1 - d], recv.at[8])
+            landed(pair_out.at[pl.ds(0, 48)], send.at[8])
+            landed(pair_out.at[pl.ds(0, 48)], recv.at[8])
 
     def prepare():
         flags = genuine[...].astype(F32)
@@ -141,14 +142,14 @@
         offset[...] = column_of(offset_row[...], 128)
         tri_gain[...] = column_of(tri_gain_row[...], 128)
         res_gain[...] = column_of(res_gain_row[...], 128)
-        score_t[...] = score[...].T * score_gain[...]
+        score_t[...] = score[...] * score_gain[...]
         tri_t[...] = tri[...].astype(F32).T.astype(BF16)
         res_t[...] = res[...].astype(F32).T.astype(BF16)
         row, col = iota(256, 256, 0), iota(256, 256, 1)
         same = row // 64 == lax.rem(col // 32, 4)
         same_t = lax.rem(row // 32, 4) == col // 64
         spread = (iota(64, 256, 0) == lax.rem(iota(64, 256, 1), 64)).astype(BF16)
-        out4 = nn(out_w[...], spread).astype(BF16)
+        out4 = tn(out_w[...], spread).astype(BF16)
         for hp in range(4):
             pick = (row == (2 * hp + col // 128) * 32 + lax.rem(col, 32)).astype(BF16)
             for w, out in ((content, val_bd), (gate_w, gate_bd)):
@@ -206,8 +207,9 @@
     pl.semaphore_wait(plane_sem, NR - 1)
 
     c_t = r * 4 + c // 4
-    r_dst = r_buf.at[pl.ds(pl.multiple_of(lax.rem(c, 4) * 192, 192), 192), lane_half]
-    self_r = c_t == c
+    m_src = lax.rem(c, 4)
+    r_dst = r_buf.at[pl.ds(pl.multiple_of(m_src * 192, 192), 192), lane_half]
+    self_r = jnp.logical_and(c_t == c, m_src == r)
 
     @pl.when(self_r)
     def _():
@@ -215,15 +217,12 @@
 
     @pl.when(jnp.logical_not(self_r))
     def _():
-        remote(r_msg, r_dst, 1, (r, c_t, d))
-
-    def send_r(k, _):
-        remote(r_msg, r_dst, 1, (lax.rem(r + k // 2, NR), c_t, lax.rem(d + k, ND)))
-        return 0
-
-    lax.fori_loop(1, NR * ND, send_r, 0)
-
-    prepare()
+        remote(r_msg, r_dst, 1, (m_src, c_t, d))
+
+    landed(r_msg, recv.at[1])
+    r_mine = r_buf.at[pl.ds(pl.multiple_of(r * 192, 192), 192), lane_half]
+    for k in range(1, NR * ND):
+        remote(r_mine, r_mine, 11, (lax.rem(r + k // 2, NR), c, lax.rem(d + k, ND)))
 
     landed(l_buf.at[pl.ds(0, 8)], recv.at[0])
     for k in range(4):
@@ -240,14 +239,18 @@
 
     lax.fori_loop(1, 32, send_x, 0)
 
-    landed(r_buf, recv.at[1])
+    prepare()
+
+    landed(r_buf.at[pl.ds(0, 672)], recv.at[11])
     landed(l_buf.at[pl.ds(0, 8)], recv.at[9])
 
     def outer_step(k, _):
-        outer[k] = nt(r_buf[...], l_buf[k]).astype(BF16)
-        return 0
-
-    lax.fori_loop(0, 16, outer_step, 0)
+        o = nt(r_buf[...], l_buf[pl.ds(2 * k, 2)].reshape(256, 256)).astype(BF16)
+        outer[2 * k] = o[:, :128]
+        outer[2 * k + 1] = o[:, 128:]
+        return 0
+
+    lax.fori_loop(0, 8, outer_step, 0)
 
     lane = lax.broadcasted_iota(jnp.int32, (128, 128), 1)
     first = lax.rem(lane // PAD, 2) == 0
@@ -258,29 +261,37 @@
     ri = ri_mask[0:1, :]
     score_both = jnp.concatenate([score_hi, score_lo], axis=0)
 
-    def column(j, _):
-        rhs = outer[:, pl.ds(pl.multiple_of(j * 32, 32), 32), :].reshape(512, 128)
+    def columns(step, _):
+        js = [step * GROUP + g for g in range(GROUP)]
+        parts = [slice(g * 128, (g + 1) * 128) for g in range(GROUP)]
+        wide = lambda blocks: jnp.concatenate(blocks, axis=1)
+        rhs = wide([outer[:, pl.ds(pl.multiple_of(j * 32, 32), 32), :].reshape(512, 128) for j in js])
         o = nn(final_t[...], rhs)
-        t = jnp.where(first, o[:128], o[128:])
-        u = t + jnp.where(first, pltpu.roll(t, 120, 1), pltpu.roll(t, 8, 1))
-        one = (couple[j].astype(F32) + (u * inv_count + offset[...])).astype(BF16)
-        pair[j] = one
-        x = normed_rows(one.astype(F32))
-        x_hi, x_lo = split2(x)
-        two = nn(score_both, x_hi)
-        flag = cj_flag[pl.ds(j, 1), :]
-        lg = two[:8] + two[8:] + nn(score_hi, x_lo) + 1e9 * (flag - 1.0)
-        m = j // TOK
-        row = lax.rem(m, 2) * 16 + (m // 2) * PAD + lax.rem(j, TOK)
-        logit[pl.ds(row, 4, stride=32), :] = jnp.where(first4, lg[:4], lg[4:])
-        q = nn(tri_t[...], (x * tri_gain[...]).astype(BF16))
-        sg = sigmoid(jnp.where(is_left, q[0:128], q[256:384]))
-        tri = sg * jnp.where(is_left, q[128:256], q[384:512]) * (flag * ri)
-        tri_f32[pl.ds(j, 128, stride=COLS), :] = tri
-        gate4[j] = sigmoid(q[512:640])
-        return 0
-
-    lax.fori_loop(0, COLS, column, 0)
+        xs = []
+        for j, part in zip(js, parts):
+            t = jnp.where(first, o[:128, part], o[128:, part])
+            u = t + jnp.where(first, pltpu.roll(t, 120, 1), pltpu.roll(t, 8, 1))
+            one = (couple[j].astype(F32) + (u * inv_count + offset[...])).astype(BF16)
+            pair[j] = one
+            xs.append(normed_rows(one.astype(F32)))
+        his, los = zip(*[split2(x) for x in xs])
+        two = nn(score_both, wide(his))
+        lgs = two[:8] + two[8:] + nn(score_hi, wide(los))
+        qs = nn(tri_t[...], wide([(x * tri_gain[...]).astype(BF16) for x in xs]))
+        for j, part in zip(js, parts):
+            flag = cj_flag[pl.ds(j, 1), :]
+            lg = lgs[:, part] + 1e9 * (flag - 1.0)
+            m = j // TOK
+            row = lax.rem(m, 2) * 16 + (m // 2) * PAD + lax.rem(j, TOK)
+            logit[pl.ds(row, 4, stride=32), :] = jnp.where(first4, lg[:4], lg[4:])
+            sg = sigmoid(jnp.where(is_left, qs[0:128, part], qs[256:384, part]))
+            tri_f32[pl.ds(j, 128, stride=COLS), :] = (
+                sg * jnp.where(is_left, qs[128:256, part], qs[384:512, part]) * (flag * ri)
+            )
+            gate4[j] = sigmoid(qs[512:640, part])
+        return 0
+
+    lax.fori_loop(0, COLS // GROUP, columns, 0)
 
     tri_msg[...] = tri_f32[...].reshape(128, COLS, 128).astype(BF16)
     local(tri_msg.at[me], tri_buf.at[r, c, d], 3)
@@ -418,6 +429,9 @@
     landed(z_buf, recv.at[7])
     z = z_buf[...].astype(F32)
     z_f32[...] = normed_rows(z).reshape(2048, 128)
+    row, lane = iota(96, 128, 0), iota(96, 128, 1)
+    i, high = row % 48, row // 48
+    compact = (lane == (i // TOK) * 16 + high * PAD + lax.rem(i, TOK)).astype(BF16)
     for m in range(2):
         for t in range(TOK):
             zq = z_f32[pl.ds(m * PAD + t, 128, stride=16), :] * res_gain[...]
@@ -425,8 +439,12 @@
             j0, j1 = m * TOK + t, (2 + m) * TOK + t
             one = jnp.where(first, pair[j0].astype(F32), pair[j1].astype(F32))
             g4 = jnp.where(first, gate4[j0], gate4[j1])
-            pair_out[d, m * TOK + t] = (one + g4 * f).T.astype(BF16)
-    remote(pair_out.at[d], pair_out.at[d], 8, (r, c, 1 - d))
+            by_token = nt(compact, (one + g4 * f).astype(BF16))
+            out_f32[pl.ds(j0, 48, stride=COLS), :] = by_token[:48]
+            out_f32[pl.ds(j1, 48, stride=COLS), :] = by_token[48:]
+    mine = pair_out.at[pl.ds(d * 48, 48)]
+    mine[...] = out_f32[...].reshape(48, COLS, 128).astype(BF16)
+    remote(mine, mine, 8, (r, c, 1 - d))
 
     landed(d_buf, recv.at[6])
     revised[...] = (x_blk[...].astype(F32) + d_buf[...].astype(F32)).astype(BF16)
@@ -456,9 +474,9 @@
     args = (
         x_tok, x_blk, couple, present_sequence_flags.reshape(2, 128), genuine_residue_flags.reshape(3, 128),
         row(tensor_scale), tensor_entry_matrix, tensor_final_matrix.reshape(16, 2, 32, 128), row(tensor_offset),
-        row(mean_couple_scale), mean_score_matrix, row(trimul_scale), trimul_entry_matrix,
+        row(mean_couple_scale), mean_score_matrix.T, row(trimul_scale), trimul_entry_matrix,
         row(trimul_result_scale), trimul_final_matrix, row(mean_sequence_scale),
-        mean_content_matrix, mean_sigmoid_matrix, mean_final_matrix,
+        mean_content_matrix, mean_sigmoid_matrix, mean_final_matrix.T,
     )
     V = pltpu.VMEM
     revised, pair_out = pl.pallas_call(
@@ -466,7 +484,7 @@
         name="msa_block",
         out_shape=(
             jax.ShapeDtypeStruct((8, PAD, 1024), BF16),
-            jax.ShapeDtypeStruct((2, 12, 128, 128), BF16),
+            jax.ShapeDtypeStruct((96, COLS, 128), BF16),
         ),
         in_specs=[vm] * len(args),
         out_specs=(vm, vm),
@@ -483,8 +501,8 @@
             V((NR, NC, ND, 16, 128), BF16), V((128, 16, 128), BF16), V((2048, 128), F32),
             V((8, 128), F32), V((COLS, 128), F32), V((256, 512), BF16), V((128, 128), F32), V((8, 128), F32),
             V((128, 128), F32), V((640, 128), BF16), V((128, 128), F32), V((128, 128), BF16),
-            V((4, 256, 256), BF16), V((4, 256, 256), BF16), V((4, 256, 256), BF16),
-            pltpu.SemaphoreType.DMA((11,)), pltpu.SemaphoreType.DMA((11,)),
+            V((4, 256, 256), BF16), V((4, 256, 256), BF16), V((4, 256, 256), BF16), V((48 * COLS, 128), F32),
+            pltpu.SemaphoreType.DMA((12,)), pltpu.SemaphoreType.DMA((12,)),
             pltpu.SemaphoreType.REGULAR,
         ],
         compiler_params=pltpu.CompilerParams(
@@ -493,8 +511,6 @@
     )(*args)
     revised = revised[:, :TOK].reshape(8, TOK, 16, 64)
     revised = jnp.transpose(revised, (0, 2, 1, 3)).reshape(128, TOK, 64)
-    pair_out = pair_out.reshape(2, 2, TOK, 8, 2, PAD, 128)[:, :, :, :, :, :TOK]
-    pair_out = jnp.transpose(pair_out, (0, 3, 5, 4, 1, 2, 6)).reshape(96, COLS, 128)
     return revised, pair_out
 
 

time: 103 us -> 82.4 us (0.80)
  Pallas kernels: 91.5 us -> 75.4 us
  local copies, waits for them, and re-layouts: 9.45 us -> 4.87 us
    pallas_call x1, Pallas kernels: 91.5 us -> 75.4 us  [on_device(): pl.pallas_call(kernel, name='msa_block', out_shape=(jax.ShapeDtypeStruct(...]
    unnamed x7, local copies, waits for them, and re-layouts: 6.34 us -> 2.72 us
where the time goes in v3:
time: 82.4 us; the launch traced here: 82.2 us
  Pallas kernels  75.4 us (92%)
  local copies, waits for them, and re-layouts  4.87 us (6%)
  matrix products  1.32 us (2%)
    pallas_call x1, Pallas kernels, on_device(): pl.pallas_call(kernel, name='msa_block', out_shape=(jax.ShapeDtypeStruct(...  75.4 us
    unnamed x7, local copies, waits for them, and re-layouts  2.72 us

profile of v3, /device:TPU:1, one launch (start us, length us, event | category | flops | bytes accessed | tf_op | source)
XLA Modules:
  0.0 82.2 jit_solution(13103232623036412414)
XLA Ops:
  0.6 0.0 copy-start
  0.7 1.1 %copy.23 = bf16[128,6,64]{2,0,1:T(8,128)(2,1)S(1)} copy(bf16[128,6,64]{0,2,1:T(8,128)(2,1)} %param.18) | data formatting | bytes 196608 | tf_op args[0]
  1.8 0.2 reshape.68
  2.0 0.1 copy.24
  2.0 0.7 pad.4.x_blk
  2.7 0.0 copy-done
  2.7 1.3 %convolution_convert_fusion.couple = bf16[24,128,128]{2,1,0:T(8,128)(2,1)} fusion(bf16[48,24,128]{2,1,0:T(8,128)(2,1)S(1)} %constant_dynamic-slice_fusion, s32[128]{0:T(128)S(1)} %compare_select_fusion), kind=kOutput, calls=%fused_computation | convolution fusion | flops 38148096 | bytes 1081856 | tf_op jit(solution)/shard_map/ijc,ip->jcp/dot_general | solution.py:471
  4.1 75.4 %msa_block.1 = (bf16[8,8,1024]{2,1,0:T(8,128)(2,1)}, bf16[96,24,128]{2,1,0:T(8,128)(2,1)}) custom-call(bf16[6,64,128]{2,1,0:T(8,128)(2,1)} %bitcast.30, bf16[8,8,1024]{2,1,0:T(8,128)(2,1)} %pad.4.x_blk, bf16[24,128,128]{2,1,0:T(8,128)(2,1)} %convolution_convert_fusion.couple, s32[2,128]{1,0:T(2,128)} %bitcast.36, s32[3,128]{1,0:T(4,128)} %bitcast.35, ...), custom_call_target="tpu_custom_call" | custom-call | tf_op jit(solution)/shard_map/msa_block/pallas_call | solution.py:482
  79.4 0.0 copy-start.1
  79.4 1.0 %copy.26 = bf16[8,6,1024]{2,0,1:T(8,128)(2,1)S(1)} copy(bf16[8,6,1024]{2,1,0:T(8,128)(2,1)} %bitcast.32) | data formatting | bytes 196608 | tf_op jit(solution)/shard_map/slice | solution.py:512
  80.5 0.2 reshape.78
  80.6 0.8 copy.27
  81.4 0.0 copy-done.1
  81.4 0.8 copy.32
  (2 shorter events, 0.0 us)
Async XLA Ops:
  0.6 2.1 %copy-start = (bf16[96,24,128]{2,1,0:T(8,128)(2,1)S(1)}, bf16[96,24,128]{2,1,0:T(8,128)(2,1)}, u32[]{:S(2)}) copy-start(bf16[96,24,128]{2,1,0:T(8,128)(2,1)} %param.21) | copy-start | bytes 1769476
  79.4 2.0 %copy-start.1 = (bf16[96,24,128]{2,1,0:T(8,128)(2,1)S(1)}, bf16[96,24,128]{2,1,0:T(8,128)(2,1)}, u32[]{:S(2)}) copy-start(bf16[96,24,128]{2,1,0:T(8,128)(2,1)} %get-tuple-element.11) | copy-start | bytes 1769476

commit v4 on v3

--- a/solution.py
+++ b/solution.py
@@ -6,7 +6,6 @@
 from jax.experimental import pallas as pl
 from jax.experimental.pallas import tpu as pltpu
 from jax.sharding import PartitionSpec as P
-
 
 MESH = pl.DeviceIdType.MESH
 EPS = 1e-05
@@ -16,7 +15,7 @@
 ALL = NR * NC * ND
 TOK, PAD = 6, 8
 COLS = 24
-GROUP = 6
+GROUP = 8
 
 
 def nt(a, b):
@@ -66,7 +65,7 @@
     logit, p_msg, st_msg, p_buf, st_buf, x_buf, xn_buf, v_buf, d_msg, d_buf,
     tl_all, tr_all, z_msg, z_buf, z_f32,
     ri_mask, cj_flag, final_t, offset, score_t, tri_gain, tri_t, res_gain, res_t,
-    val_bd, gate_bd, out_bd, out_f32,
+    val_bd, gate_bd, out_bd, out_f32, couple_s, x_pad,
     send, recv, plane_sem,
 ):
     r = lax.axis_index("row")
@@ -90,7 +89,8 @@
         if k >= 2:
             landed(l_buf.at[pl.ds(0, 7)], send.at[0])
             landed(l_buf.at[pl.ds(0, 8)], send.at[9])
-            landed(r_buf.at[pl.ds(0, 672)], send.at[11])
+            landed(r_buf.at[pl.ds(0, 576)], send.at[11])
+            landed(r_msg, send.at[1])
             landed(x_buf.at[0, pl.ds(0, 31)], send.at[2])
         if k >= 5:
             landed(tri_msg.at[pl.ds(0, ALL - 1)], send.at[3])
@@ -120,6 +120,33 @@
         if k >= 9:
             landed(pair_out.at[pl.ds(0, 48)], send.at[8])
             landed(pair_out.at[pl.ds(0, 48)], recv.at[8])
+
+    def send_x_all():
+        x_dst = x_buf.at[core, r * 8 + c // 2]
+        local(x_pad.at[c // 2], x_dst, 2)
+
+        def send_x(k, _):
+            b = lax.rem(c // 2 + k // 4, 8)
+            remote(x_pad.at[b], x_dst, 2, (lax.rem(r + k, NR), 2 * b + core, d))
+            return 0
+
+        lax.fori_loop(1, 32, send_x, 0)
+
+    def prepare_couple():
+        out_f32[...] = couple[pl.ds(pl.multiple_of(d * 48, 48), 48)].astype(F32).reshape(48 * COLS, 128)
+        lane = iota(48, 128, 1)
+        valid = lax.rem(lane, PAD) < TOK
+        spread = jnp.logical_and(iota(48, 128, 0) == (lane // 16) * TOK + lax.rem(lane, PAD), valid)
+        spread = spread.astype(BF16)
+
+        def some(step, _):
+            for g in range(4):
+                j = step * 4 + g
+                tile = out_f32[pl.ds(j, 48, stride=COLS), :].astype(BF16)
+                couple_s[j] = tn(tile, spread).astype(BF16)
+            return 0
+
+        lax.fori_loop(0, COLS // 4, some, 0)
 
     def prepare():
         flags = genuine[...].astype(F32)
@@ -170,6 +197,7 @@
         pl.semaphore_signal(barrier, inc=1, device_id=(lax.rem(r + k, NR), c, d), device_id_type=MESH)
 
     l_f32[...] = jnp.zeros_like(l_f32)
+    x_pad[...] = jnp.pad(x_blk[...], ((0, 0), (0, PAD - TOK), (0, 0)))
     here = present[...].astype(F32)
     s_mask = jnp.where(d == 0, here[0:1], here[1:2])
     inv_count = 1.0 / (jnp.sum(here, keepdims=True).reshape(1, 1) + 0.001)
@@ -219,29 +247,22 @@
     def _():
         remote(r_msg, r_dst, 1, (m_src, c_t, d))
 
-    landed(r_msg, recv.at[1])
-    r_mine = r_buf.at[pl.ds(pl.multiple_of(r * 192, 192), 192), lane_half]
-    for k in range(1, NR * ND):
-        remote(r_mine, r_mine, 11, (lax.rem(r + k // 2, NR), c, lax.rem(d + k, ND)))
+    remote(r_msg, r_dst, 1, (m_src, c_t, 1 - d))
+    prepare_couple()
+    r_mine = r_buf.at[pl.ds(pl.multiple_of(r * 192, 192), 192)]
+    landed(r_mine, recv.at[1])
+    for k in range(1, NR):
+        remote(r_mine, r_mine, 11, (lax.rem(r + k, NR), c, d))
 
     landed(l_buf.at[pl.ds(0, 8)], recv.at[0])
     for k in range(4):
         block = l_buf.at[:, pl.ds(pl.multiple_of((2 * k + core) * 16, 16), 16), :]
         remote(block, block, 9, sibling)
 
-    x_dst = x_buf.at[core, r * 8 + c // 2]
-    local(x_blk.at[c // 2], x_dst, 2)
-
-    def send_x(k, _):
-        b = lax.rem(c // 2 + k // 4, 8)
-        remote(x_blk.at[b], x_dst, 2, (lax.rem(r + k, NR), 2 * b + core, d))
-        return 0
-
-    lax.fori_loop(1, 32, send_x, 0)
-
+    send_x_all()
     prepare()
 
-    landed(r_buf.at[pl.ds(0, 672)], recv.at[11])
+    landed(r_buf.at[pl.ds(0, 576)], recv.at[11])
     landed(l_buf.at[pl.ds(0, 8)], recv.at[9])
 
     def outer_step(k, _):
@@ -271,7 +292,7 @@
         for j, part in zip(js, parts):
             t = jnp.where(first, o[:128, part], o[128:, part])
             u = t + jnp.where(first, pltpu.roll(t, 120, 1), pltpu.roll(t, 8, 1))
-            one = (couple[j].astype(F32) + (u * inv_count + offset[...])).astype(BF16)
+            one = (couple_s[j].astype(F32) + (u * inv_count + offset[...])).astype(BF16)
             pair[j] = one
             xs.append(normed_rows(one.astype(F32)))
         his, los = zip(*[split2(x) for x in xs])
@@ -447,7 +468,7 @@
     remote(mine, mine, 8, (r, c, 1 - d))
 
     landed(d_buf, recv.at[6])
-    revised[...] = (x_blk[...].astype(F32) + d_buf[...].astype(F32)).astype(BF16)
+    revised[...] = (x_pad[...].astype(F32) + d_buf[...].astype(F32)).astype(BF16)[:, :TOK]
 
 
     finish(9)
@@ -460,19 +481,12 @@
     mean_sigmoid_matrix, mean_final_matrix, trimul_scale, trimul_entry_matrix,
     trimul_result_scale, trimul_final_matrix,
 ):
-    d = lax.axis_index("depth")
     x_tok = jnp.transpose(sequence_stack, (1, 2, 0))
     x_blk = jnp.transpose(sequence_stack.reshape(8, 16, TOK, 64), (0, 2, 1, 3)).reshape(8, TOK, 1024)
-    x_blk = jnp.pad(x_blk, ((0, 0), (0, PAD - TOK), (0, 0)))
-    lane = jnp.arange(128)
-    place = jnp.where(lane % PAD < TOK, (lane // 16) * TOK + lane % PAD, -1)
-    spread = (jnp.arange(48)[:, None] == place[None, :]).astype(BF16)
-    mine = lax.dynamic_slice_in_dim(couple_state, d * 48, 48, 0)
-    couple = jnp.einsum("ijc,ip->jcp", mine, spread, preferred_element_type=F32).astype(BF16)
     vm = pl.BlockSpec(memory_space=pltpu.VMEM)
     row = lambda v: v.reshape(1, -1)
     args = (
-        x_tok, x_blk, couple, present_sequence_flags.reshape(2, 128), genuine_residue_flags.reshape(3, 128),
+        x_tok, x_blk, couple_state, present_sequence_flags.reshape(2, 128), genuine_residue_flags.reshape(3, 128),
         row(tensor_scale), tensor_entry_matrix, tensor_final_matrix.reshape(16, 2, 32, 128), row(tensor_offset),
         row(mean_couple_scale), mean_score_matrix.T, row(trimul_scale), trimul_entry_matrix,
         row(trimul_result_scale), trimul_final_matrix, row(mean_sequence_scale),
@@ -483,7 +497,7 @@
         kernel,
         name="msa_block",
         out_shape=(
-            jax.ShapeDtypeStruct((8, PAD, 1024), BF16),
+            jax.ShapeDtypeStruct((8, TOK, 1024), BF16),
             jax.ShapeDtypeStruct((96, COLS, 128), BF16),
         ),
         in_specs=[vm] * len(args),
@@ -501,7 +515,7 @@
             V((NR, NC, ND, 16, 128), BF16), V((128, 16, 128), BF16), V((2048, 128), F32),
             V((8, 128), F32), V((COLS, 128), F32), V((256, 512), BF16), V((128, 128), F32), V((8, 128), F32),
             V((128, 128), F32), V((640, 128), BF16), V((128, 128), F32), V((128, 128), BF16),
-            V((4, 256, 256), BF16), V((4, 256, 256), BF16), V((4, 256, 256), BF16), V((48 * COLS, 128), F32),
+            V((4, 256, 256), BF16), V((4, 256, 256), BF16), V((4, 256, 256), BF16), V((48 * COLS, 128), F32), V((COLS, 128, 128), BF16), V((8, PAD, 1024), BF16),
             pltpu.SemaphoreType.DMA((12,)), pltpu.SemaphoreType.DMA((12,)),
             pltpu.SemaphoreType.REGULAR,
         ],
@@ -509,7 +523,7 @@
             collective_id=0, has_side_effects=True, vmem_limit_bytes=56 * 1024 * 1024
         ),
     )(*args)
-    revised = revised[:, :TOK].reshape(8, TOK, 16, 64)
+    revised = revised.reshape(8, TOK, 16, 64)
     revised = jnp.transpose(revised, (0, 2, 1, 3)).reshape(128, TOK, 64)
     return revised, pair_out
 

time: 82.4 us -> 80.2 us (0.973)
  matrix products: 1.32 us -> 0 us
    dot_general x1 -> x0, matrix products: 1.32 us -> none  [on_device(): jnp.einsum('ijc,ip->jcp', mine, spread, preferred_element_type=F32)]
    pallas_call x0 -> x1, local copies, waits for them, and re-layouts: none -> 1.03 us  [on_device(): pl.pallas_call(kernel, name='msa_block', out_shape=(jax.ShapeDtypeStruct(...]
    slice x1 -> x0, local copies, waits for them, and re-layouts: 1.03 us -> none  [on_device(): revised = revised[:, :TOK].reshape(8, TOK, 16, 64)]
    unnamed x7 -> x5, local copies, waits for them, and re-layouts: 2.72 us -> 2.65 us
where the time goes in v4:
time: 80.2 us; the launch traced here: 80 us
  Pallas kernels  74.6 us (93%)
  local copies, waits for them, and re-layouts  4.74 us (6%)
    pallas_call x1, Pallas kernels, on_device(): pl.pallas_call(kernel, name='msa_block', out_shape=(jax.ShapeDtypeStruct(...  74.6 us
    unnamed x5, local copies, waits for them, and re-layouts  2.65 us

profile of v4, /device:TPU:1, one launch (start us, length us, event | category | flops | bytes accessed | tf_op | source)
XLA Modules:
  0.0 80.0 jit_solution(17092314986349917980)
XLA Ops:
  0.6 1.1 %copy.22 = bf16[128,6,64]{2,0,1:T(8,128)(2,1)S(1)} copy(bf16[128,6,64]{0,2,1:T(8,128)(2,1)} %param.18) | data formatting | bytes 196608 | tf_op args[0]
  1.7 0.2 reshape.44
  1.9 0.7 copy.23.x_blk
  2.6 74.6 %msa_block.1 = (bf16[8,6,1024]{2,1,0:T(8,128)(2,1)}, bf16[96,24,128]{2,1,0:T(8,128)(2,1)}) custom-call(bf16[6,64,128]{2,1,0:T(8,128)(2,1)} %bitcast.26, bf16[8,6,1024]{2,1,0:T(8,128)(2,1)} %copy.23.x_blk, bf16[96,24,128]{2,1,0:T(8,128)(2,1)} %couple.1, s32[2,128]{1,0:T(2,128)} %bitcast.31, s32[3,128]{1,0:T(4,128)} %bitcast.30, f32[1,64]{1,0:T(1,128)} %bitcast.32, ...), custom_call_target="tpu_custom_call" | custom-call | tf_op jit(solution)/shard_map/msa_block/pallas_call | solution.py:496
  77.2 0.0 copy-start
  77.2 1.0 %copy.24 = bf16[8,6,1024]{2,0,1:T(8,128)(2,1)S(1)} copy(bf16[8,6,1024]{2,1,0:T(8,128)(2,1)} %get-tuple-element.4) | data formatting | bytes 196608 | tf_op jit(solution)/shard_map/msa_block/pallas_call | solution.py:496
  78.2 0.2 reshape.54
  78.4 0.8 copy.25
  79.2 0.0 copy-done
  79.2 0.8 %copy.27 = bf16[96,24,128]{2,1,0:T(8,128)(2,1)} copy(bf16[96,24,128]{2,1,0:T(8,128)(2,1)S(1)} %copy-done) | data formatting | bytes 1179648
Async XLA Ops:
  77.2 2.0 %copy-start = (bf16[96,24,128]{2,1,0:T(8,128)(2,1)S(1)}, bf16[96,24,128]{2,1,0:T(8,128)(2,1)}, u32[]{:S(2)}) copy-start(bf16[96,24,128]{2,1,0:T(8,128)(2,1)} %get-tuple-element.11) | copy-start | bytes 1769476
